TPU v7x, 512 devices: a whole 4x8x8 slice. The times are simulated.
512 devices in a mesh: seq: 64 (over y, z), head: 8 (over x, core).
Axes of the slice: x: 4, y: 8, z: 8, core: 2. Of those that a mesh axis runs over, the one named last changes fastest.
Arguments:
- layer_input_rows: bfloat16 [8192, 4096], P('seq', 'head'), may hold values from -6 to 6
- filter_input_channels: bfloat16 [8192, 8192], P('seq', 'head'), may hold values from -6 to 6
- gate_input_channels: bfloat16 [8192, 8192], P('seq', 'head'), may hold values from -6 to 6
- state_input_vectors: bfloat16 [8192, 128], P('seq'), may hold values from -3 to 3
- state_output_vectors: bfloat16 [8192, 128], P('seq'), may hold values from -3 to 3
- decay_logarithm: float32 [8192, 64], P('seq', 'head'), may hold values from -0.7 to 0, as said below
- filter_tap_weight: bfloat16 [4, 8192], P(None, 'head'), may hold values from -3 to 3
- head_skip_gain: float32 [64], P('head'), may hold values from 0.5 to 1.5
- gated_norm_gain: float32 [8192], P('head'), may hold values from 0.1 to 1.9
- adapter_down_in: bfloat16 [4096, 32], P('head'), may hold values from -0.09375 to 0.09375
- adapter_up_in: bfloat16 [2, 32, 8192], P(None, None, 'head'), may hold values from -1 to 1
- adapter_down_out: bfloat16 [8192, 32], P('head'), may hold values from -0.0625 to 0.0625
- adapter_up_out: bfloat16 [32, 4096], P(None, 'head'), may hold values from -1 to 1
- output_gradient: bfloat16 [8192, 4096], P('seq', 'head'), may hold values from -6 to 6
- base_path_gradient: bfloat16 [8192, 8192], P('seq', 'head'), may hold values from -6 to 6
Outputs:
- grad_conv_in: bfloat16 [8192, 8192], P('seq', 'head')
- grad_gate_in: bfloat16 [8192, 8192], P('seq', 'head')
- grad_state_b: float32 [8192, 128], P(('seq', 'head'))
- grad_state_c: float32 [8192, 128], P(('seq', 'head'))
- grad_log_decay: float32 [8192, 64], P('seq', 'head')
- grad_layer_in: bfloat16 [8192, 4096], P('seq', 'head')
- grad_lora_a_in: float32 [4096, 32], P('head')
- grad_lora_b_in: float32 [2, 32, 8192], P(None, None, 'head')
- grad_lora_a_out: float32 [8192, 32], P('head')
- grad_lora_b_out: float32 [32, 4096], P(None, 'head')
Inputs may be any that keep to these rules, and one draw needn't show every extreme that they name: `decay_logarithm`: each entry is the logarithm of a decay factor between 0 and 1.
All inputs are finite; a program needn't handle non-finite values.
Results may differ from a plain program's by a relative error of at most 0.0017.
Values may be sent and summed in bfloat16 or wider, within the bound.
A program may use at most 128 MiB of HBM per device.

v0:
```python
import jax
import jax.numpy as jnp
from jax import lax
from jax.sharding import PartitionSpec as P

HDIM = 128
NSTATE = 128
BLOCK = 256


PRECISE_PRODUCT = lax.Precision.HIGHEST
ADAPTER_SCALE = 2.0
NORM_EPS = 1e-05


def passed_along(x, axis, by):
    devices = lax.axis_size(axis)
    pairs = [(i, i + by) for i in range(devices) if 0 <= i + by < devices]
    return lax.ppermute(x, axis, pairs)


def prefix(part, axis, combine, identity, reverse):
    count = lax.axis_size(axis)
    place = lax.axis_index(axis)
    ahead = count - 1 - place if reverse else place
    gathered = jax.tree.map(lambda a: lax.all_gather(a, axis), part)
    state = jax.tree.map(lambda a, e: jnp.zeros_like(a) + jnp.asarray(e, a.dtype), part, identity)

    def one(turn, state):
        source = count - 1 - turn if reverse else turn
        return combine(
            state, jax.tree.map(lambda a: lax.dynamic_index_in_dim(a, source, 0, False), gathered)
        )

    return lax.fori_loop(0, ahead, one, state)


def block_pass(activated, b_float, c_float, logarithm_increments, start_state, block_rows):
    tok_rows, head_count, head_width = activated.shape
    block_count = tok_rows // block_rows
    state_width = b_float.shape[1]
    causal = (jnp.arange(block_rows)[:, None] >= jnp.arange(block_rows)[None, :])[None, :, :]

    def advance(carried_state, block_items):
        x_block, b_block, c_block, l_block = block_items
        cum_decay = jnp.cumsum(l_block, axis=0)
        cum_heads = cum_decay.T
        decay_gap = jnp.where(causal, cum_heads[:, :, None] - cum_heads[:, None, :], 0.0)
        decays = jnp.where(causal, jnp.exp(decay_gap), 0.0)
        scores = jnp.dot(c_block, b_block.T, precision=PRECISE_PRODUCT)
        weights = decays * scores[None, :, :]
        inner_out = jnp.einsum("hts,shp->thp", weights, x_block, precision=PRECISE_PRODUCT)
        outer_out = jnp.exp(cum_decay)[:, :, None] * jnp.einsum(
            "tn,hnp->thp", c_block, carried_state, precision=PRECISE_PRODUCT
        )
        to_end = jnp.exp(cum_decay[-1][None, :] - cum_decay)
        fresh_state = jnp.einsum(
            "sn,shp->hnp", b_block, x_block * to_end[:, :, None], precision=PRECISE_PRODUCT
        )
        next_state = jnp.exp(cum_decay[-1])[:, None, None] * carried_state + fresh_state
        return (next_state, inner_out + outer_out)

    block_items = (
        activated.reshape(block_count, block_rows, head_count, head_width),
        b_float.reshape(block_count, block_rows, state_width),
        c_float.reshape(block_count, block_rows, state_width),
        logarithm_increments.reshape(block_count, block_rows, head_count),
    )
    end_state, outputs = lax.scan(advance, start_state, block_items)
    return (outputs.reshape(tok_rows, head_count, head_width), end_state)


def carried(c_float, logarithm_increments, state_in):
    cum_decay = jnp.cumsum(logarithm_increments, axis=0)
    outer_out = jnp.exp(cum_decay)[:, :, None] * jnp.einsum(
        "tn,hnp->thp", c_float, state_in, precision=PRECISE_PRODUCT
    )
    passed = jnp.exp(cum_decay[-1])[:, None, None] * state_in
    return (outer_out, passed)


def end_state(activated, b_float, logarithm_increments):
    cum_decay = jnp.cumsum(logarithm_increments, axis=0)
    to_end = jnp.exp(cum_decay[-1][None, :] - cum_decay)
    return jnp.einsum(
        "sn,shp->hnp", b_float, activated * to_end[:, :, None], precision=PRECISE_PRODUCT
    )


def chain_step(earlier, later_part):
    return (
        earlier[0] + later_part[0],
        jnp.exp(later_part[0])[:, None, None] * earlier[1] + later_part[1],
    )


def body(
    layer_input_rows,
    filter_input_channels,
    gate_input_channels,
    state_input_vectors,
    state_output_vectors,
    decay_logarithm,
    filter_tap_weight,
    head_skip_gain,
    gated_norm_gain,
    adapter_down_in,
    adapter_up_in,
    adapter_down_out,
    adapter_up_out,
    output_gradient,
    base_path_gradient,
):
    tok_rows, chan_width = filter_input_channels.shape
    head_count = decay_logarithm.shape[1]
    rim_rows = filter_tap_weight.shape[0] - 1
    block_rows = min(BLOCK, tok_rows)
    row_total_count = tok_rows * lax.axis_size("seq")
    all_channels = chan_width * lax.axis_size("head")
    taps = filter_tap_weight.astype(jnp.float32)
    before = passed_along(filter_input_channels[tok_rows - rim_rows :], "seq", 1)
    padded = jnp.concatenate([before, filter_input_channels], axis=0).astype(jnp.float32)
    pre_act = padded[0:tok_rows] * taps[0][None, :]
    for offset in range(1, rim_rows + 1):
        pre_act = pre_act + padded[offset : offset + tok_rows] * taps[offset][None, :]
    act_heads = jax.nn.silu(pre_act).reshape(tok_rows, head_count, HDIM)
    b_float = state_input_vectors.astype(jnp.float32)
    c_float = state_output_vectors.astype(jnp.float32)
    zero_state = jnp.zeros((head_count, NSTATE, HDIM), jnp.float32)
    zero_decay = jnp.zeros((head_count,), jnp.float32)

    def local_pass(activated, b_part, c_part, logarithm_increments):
        return block_pass(activated, b_part, c_part, logarithm_increments, zero_state, block_rows)

    (inner_out, fresh_state), pull_local = jax.vjp(
        local_pass, act_heads, b_float, c_float, decay_logarithm
    )
    total_decay = jnp.sum(decay_logarithm, axis=0)
    _, state_in = prefix(
        (total_decay, fresh_state), "seq", chain_step, (zero_decay, zero_state), False
    )
    (outer_out, _), pull_carry = jax.vjp(carried, c_float, decay_logarithm, state_in)
    ssd_out = inner_out + outer_out + head_skip_gain[None, :, None] * act_heads
    mixer_out = ssd_out.reshape(tok_rows, chan_width)
    gate_float = gate_input_channels.astype(jnp.float32)
    gate_sig = jax.nn.sigmoid(gate_float)
    gated_out = mixer_out * gate_float * gate_sig
    square_part = jnp.sum(gated_out * gated_out, axis=1)
    scaled = gated_out * gated_norm_gain[None, :]
    down_out_factor = adapter_down_out.astype(jnp.float32)
    square_sum = lax.psum(square_part, "head")
    inv_rms = lax.rsqrt(square_sum / all_channels + NORM_EPS)
    normed = scaled * inv_rms[:, None]
    low_out = lax.psum(jnp.dot(normed, down_out_factor, precision=PRECISE_PRODUCT), "head")
    reverse_out_grad = lax.psum(
        jnp.dot(output_gradient, adapter_up_out.T, preferred_element_type=jnp.float32), "head"
    )
    normalized_gradient = base_path_gradient.astype(jnp.float32) + ADAPTER_SCALE * jnp.dot(
        reverse_out_grad, down_out_factor.T, precision=PRECISE_PRODUCT
    )
    weighted = normalized_gradient * gated_norm_gain[None, :]
    dot_total = lax.psum(jnp.sum(weighted * gated_out, axis=1), "head")
    grad_gated = (
        inv_rms[:, None] * weighted
        - gated_out * (inv_rms * inv_rms * inv_rms * dot_total / all_channels)[:, None]
    )
    grad_mixer = grad_gated * gate_float * gate_sig
    grad_gate = grad_gated * mixer_out * gate_sig * (1.0 + gate_float * (1.0 - gate_sig))
    grad_ssd = grad_mixer.reshape(tok_rows, head_count, HDIM)
    cum_decay = jnp.cumsum(decay_logarithm, axis=0)
    local_grad = jnp.einsum(
        "tn,thp->hnp", c_float, grad_ssd * jnp.exp(cum_decay)[:, :, None], precision=PRECISE_PRODUCT
    )
    _, state_grad = prefix(
        (total_decay, local_grad), "seq", chain_step, (zero_decay, zero_state), True
    )
    grad_act, grad_b, grad_c, grad_steps = pull_local((grad_ssd, state_grad))
    carry_c, carry_steps, _ = pull_carry((grad_ssd, state_grad))
    grad_c = grad_c + carry_c
    grad_steps = grad_steps + carry_steps
    grad_act = grad_act + head_skip_gain[None, :, None] * grad_ssd
    pre_sig = jax.nn.sigmoid(pre_act)
    grad_pre = grad_act.reshape(tok_rows, chan_width) * pre_sig * (1.0 + pre_act * (1.0 - pre_sig))
    after = passed_along(grad_pre[:rim_rows], "seq", -1)
    extended = jnp.concatenate([grad_pre, after], axis=0)
    grad_conv = extended[rim_rows : rim_rows + tok_rows] * taps[0][None, :]
    for offset in range(1, rim_rows + 1):
        grad_conv = (
            grad_conv
            + extended[rim_rows - offset : rim_rows - offset + tok_rows] * taps[offset][None, :]
        )
    grad_b_rows, grad_c_rows = (
        lax.psum_scatter(grad_b, "head", scatter_dimension=0, tiled=True),
        lax.psum_scatter(grad_c, "head", scatter_dimension=0, tiled=True),
    )
    reduced_input = lax.psum(
        jnp.dot(layer_input_rows, adapter_down_in, preferred_element_type=jnp.float32), "head"
    )
    up_in_factor = adapter_up_in.astype(jnp.float32)
    back_part = jnp.dot(grad_conv, up_in_factor[0].T, precision=PRECISE_PRODUCT) + jnp.dot(
        grad_gate, up_in_factor[1].T, precision=PRECISE_PRODUCT
    )
    reverse_in_grad = lax.psum(back_part, "head")
    layer_gradient_fn = (
        ADAPTER_SCALE
        * jnp.dot(reverse_in_grad, adapter_down_in.astype(jnp.float32).T, precision=PRECISE_PRODUCT)
    ).astype(jnp.bfloat16)
    averaging_scale = ADAPTER_SCALE / row_total_count
    grad_a_in, grad_b_in, grad_a_out, grad_b_out = lax.psum(
        (
            averaging_scale
            * jnp.dot(
                layer_input_rows.astype(jnp.float32).T, reverse_in_grad, precision=PRECISE_PRODUCT
            ),
            averaging_scale
            * jnp.stack(
                [
                    jnp.dot(reduced_input.T, grad_conv, precision=PRECISE_PRODUCT),
                    jnp.dot(reduced_input.T, grad_gate, precision=PRECISE_PRODUCT),
                ]
            ),
            averaging_scale * jnp.dot(normed.T, reverse_out_grad, precision=PRECISE_PRODUCT),
            averaging_scale
            * jnp.dot(low_out.T, output_gradient.astype(jnp.float32), precision=PRECISE_PRODUCT),
        ),
        "seq",
    )
    return (
        grad_conv.astype(jnp.bfloat16),
        grad_gate.astype(jnp.bfloat16),
        grad_b_rows,
        grad_c_rows,
        grad_steps,
        layer_gradient_fn,
        grad_a_in,
        grad_b_in,
        grad_a_out,
        grad_b_out,
    )


def solution(mesh):
    in_specs = (
        P("seq", "head"),
        P("seq", "head"),
        P("seq", "head"),
        P("seq", None),
        P("seq", None),
        P("seq", "head"),
        P(None, "head"),
        P("head"),
        P("head"),
        P("head", None),
        P(None, None, "head"),
        P("head", None),
        P(None, "head"),
        P("seq", "head"),
        P("seq", "head"),
    )
    out_specs = (
        P("seq", "head"),
        P("seq", "head"),
        P(("seq", "head"), None),
        P(("seq", "head"), None),
        P("seq", "head"),
        P("seq", "head"),
        P("head", None),
        P(None, None, "head"),
        P("head", None),
        P(None, "head"),
    )
    return jax.shard_map(body, mesh=mesh, in_specs=in_specs, out_specs=out_specs, check_vma=False)
```

profile of v0, /device:TPU:6, one launch (start us, length us, event | category | flops | bytes accessed | tf_op | source)
XLA Modules:
  0.0 900.3 jit_solution(9360454591310786965)
XLA Ops:
  8.1 4.3 collective-permute-start
  22.1 151.3 %all-reduce.3 = f32[512]{0:T(512)S(1)} all-reduce(f32[512]{0:T(512)S(1)} %dynamic-update-slice), channel_id=2, replica_groups=mesh['seq'=64,'head'=8] {'seq'}, use_global_device_ids=true, to_apply=%add.3 | all-reduce | flops 512 | bytes 4096
  175.5 21.5 %psum.71 = f32[128,32]{0,1:T(8,128)} all-reduce(f32[128,32]{0,1:T(8,128)S(1)} %fusion.89), channel_id=1, replica_groups=mesh['seq'=64,'head'=8] {'head'}, use_global_device_ids=true, to_apply=%region_6.7 | all-reduce | flops 4096 | bytes 32768 | tf_op jit(solution)/shard_map/psum | solution.py:155
  199.2 48.2 %all-gather.6.cloned.1.call-done = f32[512,128,128]{2,1,0:T(8,128)} async-done(((f32[8,128,128]{2,1,0:T(8,128)}), f32[512,128,128]{2,1,0:T(8,128)}) %all-gather.6.cloned.1.call-update) | async-done | bytes 33554448 | tf_op jit(solution)/shard_map/all_gather | solution.py:26
  249.4 2.1 fusion.6
  251.7 3.2 multiply_reduce_fusion.7
  254.9 11.1 %all-reduce.6 = (f32[128]{0:T(128)}, f32[128]{0:T(128)}) all-reduce(f32[128]{0:T(128)} %get-tuple-element.524, f32[128]{0:T(128)} %get-tuple-element.523), channel_id=1, replica_groups=mesh['seq'=64,'head'=8] {'head'}, use_global_device_ids=true, to_apply=%region_8.9 | all-reduce | flops 256 | bytes 2048 | tf_op jit(solution)/shard_map/psum | solution.py:162
  266.8 2.8 fusion.81
  270.8 1.9 convolution_bitcast_fusion.1
  272.7 2.0 copy.140
  277.7 1.6 convolution_bitcast_fusion.9
  279.3 1.7 convolution_bitcast_fusion.8
  281.7 2.0 fusion.43
  286.1 2.2 convolution_multiply_fusion.2
  288.3 281.3 %all-gather.8.cloned.1.call-done = f32[512,128,128]{2,1,0:T(8,128)} async-done(((f32[8,128,128]{2,1,0:T(8,128)}), f32[512,128,128]{2,1,0:T(8,128)}) %all-gather.8.cloned.1.call-update) | async-done | bytes 33554448 | tf_op jit(solution)/shard_map/all_gather | solution.py:26
  569.7 120.5 %while.21 = (s32[]{:T(128)}, f32[8,128,128]{2,1,0:T(8,128)S(1)}, s32[]{:T(128)}, f32[64,8]{1,0:T(8,128)}, f32[64,8,128,128]{3,2,1,0:T(8,128)}, /*index=5*/s32[]{:T(128)}, s32[]{:T(128)}, s32[]{:T(128)}, s32[]{:T(128)}) while((s32[]{:T(128)}, f32[8,128,128]{2,1,0:T(8,128)S(1)}, s32[]{:T(128)}, f32[64,8]{1,0:T(8,128)}, ...), condition=%wide.region_10.11_spmd, body=%wide.region_9.10_spmd.sunk | while | flops 262150 | bytes 1573115 | solution.py:35
  690.4 1.7 convolution_bitcast_fusion.10
  693.8 1.6 fusion.2
  699.1 3.5 collective-permute-done.1
  702.6 1.7 fusion.83
  706.7 21.9 %all-reduce.5 = (f32[128,32]{0,1:T(8,128)S(1)}, f32[128,32]{0,1:T(8,128)S(1)}, f32[128,32]{0,1:T(8,128)S(1)}) all-reduce(f32[128,32]{0,1:T(8,128)S(1)} %convolution_add_fusion.3, f32[128,32]{0,1:T(8,128)} %fusion.90, f32[128,32]{0,1:T(8,128)S(1)} %fusion.41), channel_id=1, replica_groups=mesh['seq'=64,'head'=8] {'head'}, use_global_device_ids=true, to_apply=%region_24.25 | all-reduce | flops 12288 | bytes 98304 | tf_op jit(solution)/shard_map/psum | solution.py:203
  736.6 1.7 fusion.7
  738.4 149.3 %all-reduce.9.cloned.1.call-done = (f32[512,32]{0,1:T(8,128)}, f32[2,32,1024]{2,1,0:T(8,128)}, f32[1024,32]{0,1:T(8,128)}, f32[32,512]{1,0:T(8,128)}) async-done(((f32[512,32]{0,1:T(8,128)}, f32[2,32,1024]{2,1,0:T(8,128)}, f32[1024,32]{0,1:T(8,128)}, f32[32,512]{1,0:T(8,128)}), (f32[512,32]{0,1:T(8,128)}, f32[2,32,1024]{2,1,0:T(8,128)}, f32[1024,32]{0,1:T(8,128)}, ...) | async-done | bytes 524304 | tf_op jit(solution)/shard_map/psum | solution.py:209
  889.1 1.7 copy.192
  (237 shorter events, 163.5 us)
Async XLA Ops:
  7.2 167.5 %copy-start = (bf16[128,512]{1,0:T(8,128)(2,1)S(1)}, bf16[128,512]{1,0:T(8,128)(2,1)}, u32[]{:S(2)}) copy-start(bf16[128,512]{1,0:T(8,128)(2,1)} %param.32) | copy-start | bytes 393220
  7.2 276.5 %copy-start.4 = (bf16[128,128]{1,0:T(8,128)(2,1)S(1)}, bf16[128,128]{1,0:T(8,128)(2,1)}, u32[]{:S(2)}) copy-start(bf16[128,128]{1,0:T(8,128)(2,1)} %param.22) | copy-start | bytes 98308
  7.2 685.7 %copy-start.3 = (bf16[128,128]{1,0:T(8,128)(2,1)S(1)}, bf16[128,128]{1,0:T(8,128)(2,1)}, u32[]{:S(2)}) copy-start(bf16[128,128]{1,0:T(8,128)(2,1)} %param.23) | copy-start | bytes 98308
  7.2 269.0 %copy-start.5 = (bf16[128,512]{1,0:T(8,128)(2,1)S(1)}, bf16[128,512]{1,0:T(8,128)(2,1)}, u32[]{:S(2)}) copy-start(bf16[128,512]{1,0:T(8,128)(2,1)} %param.19) | copy-start | bytes 393220
  7.2 240.2 %all-gather.6.cloned.1.call-start = ((), (), s32[]{:S(2)}) async-start(), calls=%async_computation.4 | async-start | bytes 34078720 | tf_op jit(solution)/shard_map/all_gather | solution.py:26
  8.1 6.5 collective-permute-start
  13.2 3.5 copy-start.10
  13.2 3.5 copy-start.11
  13.2 3.5 copy-start.12
  13.2 3.5 copy-start.13
  14.2 159.3 %copy-start.9 = (f32[128,8]{0,1:T(8,128)}, f32[128,8]{0,1:T(8,128)S(1)}, u32[]{:S(2)}) copy-start(f32[128,8]{0,1:T(8,128)S(1)} %copy.132) | copy-start | bytes 12292
  14.5 182.6 %copy-start.6 = (f32[128,8]{0,1:T(8,128)}, f32[128,8]{0,1:T(8,128)S(1)}, u32[]{:S(2)}) copy-start(f32[128,8]{0,1:T(8,128)S(1)} %get-tuple-element.573) | copy-start | bytes 12292
  14.5 237.0 %copy-start.8 = (f32[128,8]{0,1:T(8,128)}, f32[128,8]{0,1:T(8,128)S(1)}, u32[]{:S(2)}) copy-start(f32[128,8]{0,1:T(8,128)S(1)} %get-tuple-element.574) | copy-start | bytes 12292
  19.1 550.6 %all-gather.8.cloned.1.call-start = ((), (), s32[]{:S(2)}) async-start(), calls=%async_computation.5 | async-start | bytes 34078720 | tf_op jit(solution)/shard_map/all_gather | solution.py:26
  173.6 78.0 %copy-start.7 = (f32[8,128]{1,0:T(8,128)}, f32[8,128]{1,0:T(8,128)S(1)}, u32[]{:S(2)}) copy-start(f32[8,128]{1,0:T(8,128)S(1)} %copy.129) | copy-start | bytes 12292
  247.5 0.6 copy-start.14
  251.7 15.0 %copy-start.2 = (f32[128,1024]{1,0:T(8,128)}, f32[128,1024]{1,0:T(8,128)S(1)}, u32[]{:S(2)}) copy-start(f32[128,1024]{1,0:T(8,128)S(1)} %copy.138) | copy-start | bytes 1572868
  254.9 14.6 %copy-start.1 = (f32[128,1024]{1,0:T(8,128)}, f32[128,1024]{1,0:T(8,128)S(1)}, u32[]{:S(2)}) copy-start(f32[128,1024]{1,0:T(8,128)S(1)} %get-tuple-element.560) | copy-start | bytes 1572868
  266.7 2.8 copy-start.15
  274.8 463.6 %reduce-scatter.5.cloned.1.call-start = ((), (), s32[]{:S(2)}) async-start(), calls=%async_computation.3 | async-start | bytes 73728 | tf_op jit(solution)/shard_map/reduce_scatter | solution.py:194
  288.3 450.1 %reduce-scatter.3.cloned.1.call-start = ((), (), s32[]{:S(2)}) async-start(), calls=%async_computation.2 | async-start | bytes 73728 | tf_op jit(solution)/shard_map/reduce_scatter | solution.py:193
  697.0 5.6 collective-permute-start.1
  699.1 188.6 %all-reduce.9.cloned.1.call-start = ((), (), s32[]{:S(2)}) async-start(), calls=%async_computation.6 | async-start | bytes 1048576 | tf_op jit(solution)/shard_map/psum | solution.py:209
Sparse Core Ops, SparseCore 0:
  19.2 228.1 all-gather.5
  274.9 294.6 all-gather.7
  573.0 30.7 reduce-scatter.4
  699.2 25.5 reduce-scatter.2
  732.0 155.6 all-reduce.8
where the time goes:
time: 907 us; the launch traced here: 900 us
  waiting for transfers between devices  482 us (53%)
  blocking collectives  206 us (23%)
  other arithmetic  90.8 us (10%)
  local copies, waits for them, and re-layouts  63.6 us (7%)
  matrix products  35.3 us (4%)
  between operations  14.8 us (2%)
    all_gather x2, waiting for transfers between devices, prefix(): gathered = jax.tree.map(lambda a: lax.all_gather(a, axis), part)  330 us
    unnamed x1, blocking collectives  151 us
    psum x1, waiting for transfers between devices, body(): lax.psum((averaging_scale * jnp.dot(layer_input_rows.astype(jnp.float32)....  149 us
    add x63, other arithmetic, chain_step(): jnp.exp(later_part[0])[:, None, None] * earlier[1] + later_part[1]  74.8 us
    exp x63, local copies, waits for them, and re-layouts, chain_step(): jnp.exp(later_part[0])[:, None, None] * earlier[1] + later_part[1]  44 us
    psum x1, blocking collectives, body(): reverse_in_grad = lax.psum(back_part, 'head')  21.9 us
    psum x1, blocking collectives, body(): lax.psum(jnp.dot(output_gradient, adapter_up_out.T, preferred_element_typ...  21.5 us
  transfers between devices with their start and end apart: 7, of which 4 were waited for; matrix products, arithmetic and copies ran while one was open for 18% of the time, Pallas kernels for 0%

commit v1 on v0

--- a/solution.py
+++ b/solution.py
@@ -1,38 +1,284 @@
+import functools
+
 import jax
 import jax.numpy as jnp
 from jax import lax
+from jax.experimental import pallas as pl
+from jax.experimental.pallas import tpu as pltpu
 from jax.sharding import PartitionSpec as P
 
 HDIM = 128
 NSTATE = 128
 BLOCK = 256
+SIDE = 8
+SLICE = NSTATE // SIDE
+MESH = pl.DeviceIdType.MESH
+F32 = jnp.float32
 
 
 PRECISE_PRODUCT = lax.Precision.HIGHEST
 ADAPTER_SCALE = 2.0
 NORM_EPS = 1e-05
+
+
+def vmem():
+    return pl.BlockSpec(memory_space=pltpu.VMEM)
+
+
+def along(kind, step):
+    if kind == "head":
+        place = lax.rem(lax.axis_index("head") + step, SIDE)
+        return {"head": place}, place
+    seq = lax.axis_index("seq")
+    row, col = seq // SIDE, lax.rem(seq, SIDE)
+    if kind == "z":
+        place = lax.rem(col + step, SIDE)
+        return {"seq": row * SIDE + place}, place
+    place = lax.rem(row + step, SIDE)
+    return {"seq": place * SIDE + col}, place
+
+
+def own_place(kind):
+    if kind == "head":
+        return lax.axis_index("head")
+    seq = lax.axis_index("seq")
+    return lax.rem(seq, SIDE) if kind == "z" else seq // SIDE
+
+
+def greet(kinds):
+    barrier = pltpu.get_barrier_semaphore()
+    for kind in kinds:
+        for step in range(1, SIDE):
+            pl.semaphore_signal(
+                barrier, inc=1, device_id=along(kind, step)[0], device_id_type=MESH
+            )
+    pl.semaphore_wait(barrier, (SIDE - 1) * len(kinds))
+
+
+def exchange(kind, source, target, send_sem, recv_sem):
+    copies = []
+    for step in range(1, SIDE):
+        device, place = along(kind, step)
+        copy = pltpu.make_async_remote_copy(
+            src_ref=source(place),
+            dst_ref=target,
+            send_sem=send_sem.at[step],
+            recv_sem=recv_sem.at[step],
+            device_id=device,
+            device_id_type=MESH,
+        )
+        copy.start()
+        copies.append(copy)
+    return copies
+
+
+def arrived(copies):
+    for copy in copies:
+        copy.wait_recv()
+
+
+def left(copies):
+    for copy in copies:
+        copy.wait_send()
+
+
+def fold_kernel(
+    reverse, own_ref, out_ref, row_in, row_out, part_out, part_in, enter_out, enter_in,
+    row_mix, send_sem, recv_sem,
+):
+    row, col = own_place("y"), own_place("z")
+    order = list(range(SIDE))[::-1] if reverse else list(range(SIDE))
+    greet(("z", "y"))
+    to_owner = exchange(
+        "z", lambda place: own_ref.at[place], row_in.at[col], send_sem.at[0], recv_sem.at[0]
+    )
+    row_in[col] = own_ref[col]
+    arrived(to_owner)
+    state = jnp.zeros((NSTATE, HDIM), F32)
+    total = jnp.zeros((8, HDIM), F32)
+    for place in order:
+        row_out[place] = state
+        row_mix[place] = jnp.exp(total)
+        step = row_in[place, NSTATE : NSTATE + 8]
+        total = total + step
+        state = jnp.exp(step[0:1]) * state + row_in[place, 0:NSTATE]
+    for place in range(SIDE):
+        part_out[place, 0:SLICE] = state[place * SLICE : (place + 1) * SLICE]
+        part_out[place, SLICE : SLICE + 8] = total
+    to_part = exchange(
+        "y", lambda place: part_out.at[place], part_in.at[row], send_sem.at[1], recv_sem.at[1]
+    )
+    part_in[row] = part_out[row]
+    arrived(to_part)
+    part = jnp.zeros((SLICE, HDIM), F32)
+    for place in order:
+        enter_out[place] = part
+        part = jnp.exp(part_in[place, SLICE : SLICE + 1]) * part + part_in[place, 0:SLICE]
+    to_row = exchange(
+        "y", lambda place: enter_out.at[place], enter_in.at[row], send_sem.at[2], recv_sem.at[2]
+    )
+    enter_in[row] = enter_out[row]
+    arrived(to_row)
+    enter = enter_in[...].reshape(NSTATE, HDIM)
+    for place in range(SIDE):
+        row_out[place] = row_out[place] + row_mix[place, 0:1] * enter
+    to_all = exchange(
+        "z", lambda place: row_out.at[place], out_ref.at[col], send_sem.at[3], recv_sem.at[3]
+    )
+    out_ref[col] = row_out[col]
+    arrived(to_all)
+    for copies in (to_owner, to_part, to_row, to_all):
+        left(copies)
+
+
+def fold(states, total_decay, reverse, collective_id):
+    tail = jnp.broadcast_to(total_decay[:, None, None], (SIDE, 8, HDIM))
+    return pl.pallas_call(
+        functools.partial(fold_kernel, reverse),
+        out_shape=jax.ShapeDtypeStruct((SIDE, NSTATE, HDIM), F32),
+        in_specs=[vmem()],
+        out_specs=vmem(),
+        scratch_shapes=[
+            pltpu.VMEM((SIDE, NSTATE + 8, HDIM), F32),
+            pltpu.VMEM((SIDE, NSTATE, HDIM), F32),
+            pltpu.VMEM((SIDE, SLICE + 8, HDIM), F32),
+            pltpu.VMEM((SIDE, SLICE + 8, HDIM), F32),
+            pltpu.VMEM((SIDE, SLICE, HDIM), F32),
+            pltpu.VMEM((SIDE, SLICE, HDIM), F32),
+            pltpu.VMEM((SIDE, 8, HDIM), F32),
+            pltpu.SemaphoreType.DMA((4, SIDE)),
+            pltpu.SemaphoreType.DMA((4, SIDE)),
+        ],
+        compiler_params=pltpu.CompilerParams(collective_id=collective_id, has_side_effects=True),
+    )(jnp.concatenate([states, tail], axis=1))
+
+
+def head_sum_kernel(own_ref, out_ref, parts, send_sem, recv_sem):
+    me = own_place("head")
+    greet(("head",))
+    copies = exchange("head", lambda place: own_ref, parts.at[me], send_sem, recv_sem)
+    parts[me] = own_ref[...]
+    arrived(copies)
+    total = parts[0]
+    for place in range(1, SIDE):
+        total = total + parts[place]
+    out_ref[...] = total
+    left(copies)
+
+
+def head_sum(x, collective_id):
+    return pl.pallas_call(
+        head_sum_kernel,
+        out_shape=jax.ShapeDtypeStruct(x.shape, F32),
+        in_specs=[vmem()],
+        out_specs=vmem(),
+        scratch_shapes=[
+            pltpu.VMEM((SIDE,) + x.shape, F32),
+            pltpu.SemaphoreType.DMA((SIDE,)),
+            pltpu.SemaphoreType.DMA((SIDE,)),
+        ],
+        compiler_params=pltpu.CompilerParams(collective_id=collective_id, has_side_effects=True),
+    )(x)
+
+
+def head_scatter_kernel(own_ref, out_ref, parts, send_sem, recv_sem):
+    me = own_place("head")
+    greet(("head",))
+    copies = exchange("head", lambda place: own_ref.at[place], parts.at[me], send_sem, recv_sem)
+    parts[me] = own_ref[me]
+    arrived(copies)
+    total = parts[0]
+    for place in range(1, SIDE):
+        total = total + parts[place]
+    out_ref[...] = total
+    left(copies)
+
+
+def head_scatter(x, collective_id):
+    shape = x.shape[1:]
+    return pl.pallas_call(
+        head_scatter_kernel,
+        out_shape=jax.ShapeDtypeStruct(shape, F32),
+        in_specs=[vmem()],
+        out_specs=vmem(),
+        scratch_shapes=[
+            pltpu.VMEM((SIDE,) + shape, F32),
+            pltpu.SemaphoreType.DMA((SIDE,)),
+            pltpu.SemaphoreType.DMA((SIDE,)),
+        ],
+        compiler_params=pltpu.CompilerParams(collective_id=collective_id, has_side_effects=True),
+    )(x)
+
+
+def token_sum_kernel(own_ref, out_ref, z_in, y_out, y_in, y_sum, z_sum, send_sem, recv_sem):
+    row, col = own_place("y"), own_place("z")
+    greet(("z", "y"))
+    first = exchange(
+        "z", lambda place: own_ref.at[place], z_in.at[col], send_sem.at[0], recv_sem.at[0]
+    )
+    z_in[col] = own_ref[col]
+    arrived(first)
+    total = z_in[0]
+    for place in range(1, SIDE):
+        total = total + z_in[place]
+    y_out[...] = total
+    second = exchange(
+        "y", lambda place: y_out.at[place], y_in.at[row], send_sem.at[1], recv_sem.at[1]
+    )
+    y_in[row] = y_out[row]
+    arrived(second)
+    total = y_in[0]
+    for place in range(1, SIDE):
+        total = total + y_in[place]
+    y_sum[row] = total
+    third = exchange(
+        "y", lambda place: y_sum.at[row], y_sum.at[row], send_sem.at[2], recv_sem.at[2]
+    )
+    arrived(third)
+    z_sum[col] = y_sum[...]
+    fourth = exchange(
+        "z", lambda place: z_sum.at[col], z_sum.at[col], send_sem.at[3], recv_sem.at[3]
+    )
+    arrived(fourth)
+    for copies in (first, second, third, fourth):
+        left(copies)
+    out_ref[...] = z_sum[...]
+
+
+def token_sum(x, collective_id):
+    line, part = x.shape[1:], x.shape[2:]
+    return pl.pallas_call(
+        token_sum_kernel,
+        out_shape=jax.ShapeDtypeStruct(x.shape, F32),
+        in_specs=[vmem()],
+        out_specs=vmem(),
+        scratch_shapes=[
+            pltpu.VMEM((SIDE,) + line, F32),
+            pltpu.VMEM(line, F32),
+            pltpu.VMEM((SIDE,) + part, F32),
+            pltpu.VMEM((SIDE,) + part, F32),
+            pltpu.VMEM((SIDE,) + line, F32),
+            pltpu.SemaphoreType.DMA((4, SIDE)),
+            pltpu.SemaphoreType.DMA((4, SIDE)),
+        ],
+        compiler_params=pltpu.CompilerParams(collective_id=collective_id, has_side_effects=True),
+    )(x)
+
+
+def running_sum(x):
+    rows = x.shape[0]
+    lower = (jnp.arange(rows)[:, None] >= jnp.arange(rows)[None, :]).astype(F32)
+    return jnp.dot(lower, x, precision=PRECISE_PRODUCT)
+
+
+def turned_product(x, y):
+    return lax.dot_general(y, x, (((0,), (1,)), ((), ())), precision=PRECISE_PRODUCT)
 
 
 def passed_along(x, axis, by):
     devices = lax.axis_size(axis)
     pairs = [(i, i + by) for i in range(devices) if 0 <= i + by < devices]
     return lax.ppermute(x, axis, pairs)
-
-
-def prefix(part, axis, combine, identity, reverse):
-    count = lax.axis_size(axis)
-    place = lax.axis_index(axis)
-    ahead = count - 1 - place if reverse else place
-    gathered = jax.tree.map(lambda a: lax.all_gather(a, axis), part)
-    state = jax.tree.map(lambda a, e: jnp.zeros_like(a) + jnp.asarray(e, a.dtype), part, identity)
-
-    def one(turn, state):
-        source = count - 1 - turn if reverse else turn
-        return combine(
-            state, jax.tree.map(lambda a: lax.dynamic_index_in_dim(a, source, 0, False), gathered)
-        )
-
-    return lax.fori_loop(0, ahead, one, state)
 
 
 def block_pass(activated, b_float, c_float, logarithm_increments, start_state, block_rows):
@@ -43,7 +289,7 @@
 
     def advance(carried_state, block_items):
         x_block, b_block, c_block, l_block = block_items
-        cum_decay = jnp.cumsum(l_block, axis=0)
+        cum_decay = running_sum(l_block)
         cum_heads = cum_decay.T
         decay_gap = jnp.where(causal, cum_heads[:, :, None] - cum_heads[:, None, :], 0.0)
         decays = jnp.where(causal, jnp.exp(decay_gap), 0.0)
@@ -71,7 +317,7 @@
 
 
 def carried(c_float, logarithm_increments, state_in):
-    cum_decay = jnp.cumsum(logarithm_increments, axis=0)
+    cum_decay = running_sum(logarithm_increments)
     outer_out = jnp.exp(cum_decay)[:, :, None] * jnp.einsum(
         "tn,hnp->thp", c_float, state_in, precision=PRECISE_PRODUCT
     )
@@ -80,17 +326,10 @@
 
 
 def end_state(activated, b_float, logarithm_increments):
-    cum_decay = jnp.cumsum(logarithm_increments, axis=0)
+    cum_decay = running_sum(logarithm_increments)
     to_end = jnp.exp(cum_decay[-1][None, :] - cum_decay)
     return jnp.einsum(
         "sn,shp->hnp", b_float, activated * to_end[:, :, None], precision=PRECISE_PRODUCT
-    )
-
-
-def chain_step(earlier, later_part):
-    return (
-        earlier[0] + later_part[0],
-        jnp.exp(later_part[0])[:, None, None] * earlier[1] + later_part[1],
     )
 
 
@@ -127,7 +366,6 @@
     b_float = state_input_vectors.astype(jnp.float32)
     c_float = state_output_vectors.astype(jnp.float32)
     zero_state = jnp.zeros((head_count, NSTATE, HDIM), jnp.float32)
-    zero_decay = jnp.zeros((head_count,), jnp.float32)
 
     def local_pass(activated, b_part, c_part, logarithm_increments):
         return block_pass(activated, b_part, c_part, logarithm_increments, zero_state, block_rows)
@@ -136,9 +374,7 @@
         local_pass, act_heads, b_float, c_float, decay_logarithm
     )
     total_decay = jnp.sum(decay_logarithm, axis=0)
-    _, state_in = prefix(
-        (total_decay, fresh_state), "seq", chain_step, (zero_decay, zero_state), False
-    )
+    state_in = fold(fresh_state, total_decay, False, 0)
     (outer_out, _), pull_carry = jax.vjp(carried, c_float, decay_logarithm, state_in)
     ssd_out = inner_out + outer_out + head_skip_gain[None, :, None] * act_heads
     mixer_out = ssd_out.reshape(tok_rows, chan_width)
@@ -148,18 +384,49 @@
     square_part = jnp.sum(gated_out * gated_out, axis=1)
     scaled = gated_out * gated_norm_gain[None, :]
     down_out_factor = adapter_down_out.astype(jnp.float32)
-    square_sum = lax.psum(square_part, "head")
-    inv_rms = lax.rsqrt(square_sum / all_channels + NORM_EPS)
-    normed = scaled * inv_rms[:, None]
-    low_out = lax.psum(jnp.dot(normed, down_out_factor, precision=PRECISE_PRODUCT), "head")
-    reverse_out_grad = lax.psum(
-        jnp.dot(output_gradient, adapter_up_out.T, preferred_element_type=jnp.float32), "head"
-    )
+    early = head_sum(
+        jnp.concatenate(
+            [
+                lax.dot_general(
+                    adapter_up_out,
+                    output_gradient,
+                    (((1,), (1,)), ((), ())),
+                    preferred_element_type=jnp.float32,
+                ),
+                lax.dot_general(
+                    adapter_down_in,
+                    layer_input_rows,
+                    (((0,), (1,)), ((), ())),
+                    preferred_element_type=jnp.float32,
+                ),
+            ],
+            axis=0,
+        ),
+        1,
+    )
+    rank = adapter_up_out.shape[0]
+    reverse_out_grad = early[:rank].T
+    reduced_input = early[rank:].T
     normalized_gradient = base_path_gradient.astype(jnp.float32) + ADAPTER_SCALE * jnp.dot(
         reverse_out_grad, down_out_factor.T, precision=PRECISE_PRODUCT
     )
     weighted = normalized_gradient * gated_norm_gain[None, :]
-    dot_total = lax.psum(jnp.sum(weighted * gated_out, axis=1), "head")
+    late = head_sum(
+        jnp.concatenate(
+            [
+                turned_product(scaled, down_out_factor),
+                square_part[None, :],
+                jnp.sum(weighted * gated_out, axis=1)[None, :],
+                jnp.zeros((6, tok_rows), jnp.float32),
+            ],
+            axis=0,
+        ),
+        2,
+    )
+    inv_rms = lax.rsqrt(late[rank] / all_channels + NORM_EPS)
+    normed = scaled * inv_rms[:, None]
+    low_out = late[:rank].T * inv_rms[:, None]
+    dot_total = late[rank + 1]
     grad_gated = (
         inv_rms[:, None] * weighted
         - gated_out * (inv_rms * inv_rms * inv_rms * dot_total / all_channels)[:, None]
@@ -167,13 +434,11 @@
     grad_mixer = grad_gated * gate_float * gate_sig
     grad_gate = grad_gated * mixer_out * gate_sig * (1.0 + gate_float * (1.0 - gate_sig))
     grad_ssd = grad_mixer.reshape(tok_rows, head_count, HDIM)
-    cum_decay = jnp.cumsum(decay_logarithm, axis=0)
+    cum_decay = running_sum(decay_logarithm)
     local_grad = jnp.einsum(
         "tn,thp->hnp", c_float, grad_ssd * jnp.exp(cum_decay)[:, :, None], precision=PRECISE_PRODUCT
     )
-    _, state_grad = prefix(
-        (total_decay, local_grad), "seq", chain_step, (zero_decay, zero_state), True
-    )
+    state_grad = fold(local_grad, total_decay, True, 3)
     grad_act, grad_b, grad_c, grad_steps = pull_local((grad_ssd, state_grad))
     carry_c, carry_steps, _ = pull_carry((grad_ssd, state_grad))
     grad_c = grad_c + carry_c
@@ -189,42 +454,49 @@
             grad_conv
             + extended[rim_rows - offset : rim_rows - offset + tok_rows] * taps[offset][None, :]
         )
-    grad_b_rows, grad_c_rows = (
-        lax.psum_scatter(grad_b, "head", scatter_dimension=0, tiled=True),
-        lax.psum_scatter(grad_c, "head", scatter_dimension=0, tiled=True),
-    )
-    reduced_input = lax.psum(
-        jnp.dot(layer_input_rows, adapter_down_in, preferred_element_type=jnp.float32), "head"
-    )
+    own_rows = tok_rows // SIDE
+    grad_rows = head_scatter(
+        jnp.concatenate(
+            [grad_b.reshape(SIDE, own_rows, NSTATE), grad_c.reshape(SIDE, own_rows, NSTATE)], axis=1
+        ),
+        4,
+    )
+    grad_b_rows, grad_c_rows = grad_rows[:own_rows], grad_rows[own_rows:]
     up_in_factor = adapter_up_in.astype(jnp.float32)
-    back_part = jnp.dot(grad_conv, up_in_factor[0].T, precision=PRECISE_PRODUCT) + jnp.dot(
-        grad_gate, up_in_factor[1].T, precision=PRECISE_PRODUCT
-    )
-    reverse_in_grad = lax.psum(back_part, "head")
+    back_part = turned_product(grad_conv, up_in_factor[0].T) + turned_product(
+        grad_gate, up_in_factor[1].T
+    )
+    reverse_in_grad = head_sum(back_part, 5).T
     layer_gradient_fn = (
         ADAPTER_SCALE
         * jnp.dot(reverse_in_grad, adapter_down_in.astype(jnp.float32).T, precision=PRECISE_PRODUCT)
     ).astype(jnp.bfloat16)
     averaging_scale = ADAPTER_SCALE / row_total_count
-    grad_a_in, grad_b_in, grad_a_out, grad_b_out = lax.psum(
-        (
-            averaging_scale
-            * jnp.dot(
-                layer_input_rows.astype(jnp.float32).T, reverse_in_grad, precision=PRECISE_PRODUCT
-            ),
-            averaging_scale
-            * jnp.stack(
-                [
-                    jnp.dot(reduced_input.T, grad_conv, precision=PRECISE_PRODUCT),
-                    jnp.dot(reduced_input.T, grad_gate, precision=PRECISE_PRODUCT),
-                ]
-            ),
-            averaging_scale * jnp.dot(normed.T, reverse_out_grad, precision=PRECISE_PRODUCT),
-            averaging_scale
-            * jnp.dot(low_out.T, output_gradient.astype(jnp.float32), precision=PRECISE_PRODUCT),
-        ),
-        "seq",
-    )
+    wide = jnp.concatenate(
+        [
+            turned_product(layer_input_rows.astype(jnp.float32).T, reverse_in_grad),
+            jnp.dot(reduced_input.T, grad_conv, precision=PRECISE_PRODUCT),
+            jnp.dot(reduced_input.T, grad_gate, precision=PRECISE_PRODUCT),
+            turned_product(normed.T, reverse_out_grad),
+            jnp.dot(low_out.T, output_gradient.astype(jnp.float32), precision=PRECISE_PRODUCT),
+        ],
+        axis=1,
+    )
+    lanes = wide.shape[1] // SIDE // SIDE
+    pieces = averaging_scale * wide.reshape(rank, SIDE * SIDE, lanes)
+    pieces = pieces.transpose(1, 0, 2).reshape(SIDE, SIDE, rank * lanes // 128, 128)
+    summed = token_sum(pieces, 6).reshape(SIDE * SIDE, rank, lanes)
+    summed = summed.transpose(1, 0, 2).reshape(rank, wide.shape[1])
+    width = layer_input_rows.shape[1]
+    grad_a_in = summed[:, :width].T
+    grad_b_in = jnp.stack(
+        [
+            summed[:, width : width + chan_width],
+            summed[:, width + chan_width : width + 2 * chan_width],
+        ]
+    )
+    grad_a_out = summed[:, width + 2 * chan_width : width + 3 * chan_width].T
+    grad_b_out = summed[:, width + 3 * chan_width :]
     return (
         grad_conv.astype(jnp.bfloat16),
         grad_gate.astype(jnp.bfloat16),

time: 907 us -> 237 us (0.26)
  waiting for transfers between devices: 482 us -> 2.09 us
  blocking collectives: 206 us -> 0 us
  Pallas kernels: 0 us -> 172 us
  other arithmetic: 90.8 us -> 13.7 us
  local copies, waits for them, and re-layouts: 63.6 us -> 21.4 us
  matrix products: 35.3 us -> 19 us
  between operations: 14.8 us -> 1.29 us
    all_gather x2 -> x0, waiting for transfers between devices: 330 us -> none  [prefix(): gathered = jax.tree.map(lambda a: lax.all_gather(a, axis), part)]
    pallas_call x0 -> x7, Pallas kernels: none -> 172 us  [the longest x2 96.2 us: fold(): pl.pallas_call(functools.partial(fold_kernel, reverse), out_shape=jax.Sha...]
    unnamed x1 -> x0, blocking collectives: 151 us -> none
    psum x1 -> x0, waiting for transfers between devices: 149 us -> none  [body(): lax.psum((averaging_scale * jnp.dot(layer_input_rows.astype(jnp.float32)....]
    add x64 -> x0, other arithmetic: 74.8 us -> none  [the longest x63 74.8 us: chain_step(): jnp.exp(later_part[0])[:, None, None] * earlier[1] + later_part[1]]
    psum x3 -> x0, blocking collectives: 54.6 us -> none  [the longest x1 21.9 us: body(): reverse_in_grad = lax.psum(back_part, 'head')]
    exp x63 -> x0, local copies, waits for them, and re-layouts: 44 us -> none  [chain_step(): jnp.exp(later_part[0])[:, None, None] * earlier[1] + later_part[1]]
  transfers between devices with their start and end apart: 7 -> 2, of which waited for: 4 -> 1; matrix products, arithmetic and copies ran while one was open for 18% -> 2% of each run, Pallas kernels for 0% -> 4%
where the time goes in v1:
time: 237 us; the launch traced here: 235 us
  Pallas kernels  172 us (73%)
  local copies, waits for them, and re-layouts  21.4 us (9%)
  matrix products  19 us (8%)
  other arithmetic  13.7 us (6%)
  starting transfers between devices  5.57 us (2%)
    pallas_call x2, Pallas kernels, fold(): pl.pallas_call(functools.partial(fold_kernel, reverse), out_shape=jax.Sha...  96.2 us
    pallas_call x1, Pallas kernels, token_sum(): pl.pallas_call(token_sum_kernel, out_shape=jax.ShapeDtypeStruct(x.shape,...  42.8 us
    pallas_call x3, Pallas kernels, head_sum(): pl.pallas_call(head_sum_kernel, out_shape=jax.ShapeDtypeStruct(x.shape, F...  24.8 us
    unnamed x96, local copies, waits for them, and re-layouts  10.6 us
    pallas_call x1, Pallas kernels, head_scatter(): pl.pallas_call(head_scatter_kernel, out_shape=jax.ShapeDtypeStruct(shape,...  8.11 us
    ppermute x2, starting transfers between devices, passed_along(): return lax.ppermute(x, axis, pairs)  5.57 us
  transfers between devices with their start and end apart: 2, of which 1 were waited for; matrix products, arithmetic and copies ran while one was open for 2% of the time, Pallas kernels for 4%

profile of v1, /device:TPU:6, one launch (start us, length us, event | category | flops | bytes accessed | tf_op | source)
XLA Modules:
  0.0 234.9 jit_solution(4998397309785928601)
XLA Ops:
  1.4 4.3 %collective-permute-start = (bf16[3,1024]{1,0:T(4,128)(2,1)S(1)}, bf16[3,1024]{1,0:T(4,128)(2,1)S(1)}, u32[]{:S(2)}, u32[]{:S(2)}) collective-permute-start(bf16[3,1024]{1,0:T(4,128)(2,1)S(1)} %slice.97), channel_id=1, source_target_pairs={{0,8},{8,16},{16,24},{24,32},{32,40},{40,48},{48,56},{56,64},{64,7... | collective-permute-start | bytes 18440 | tf_op jit(solution)/shard_map/ppermute | solution.py:281
  10.9 8.9 %shard_map.223 = f32[64,128]{1,0:T(8,128)} custom-call(f32[64,128]{1,0:T(8,128)} %pad_maximum_fusion.5.own_ref), custom_call_target="tpu_custom_call" | custom-call | tf_op jit(solution)/shard_map/pallas_call | solution.py:170
  19.8 1.0 copy.65
  21.0 1.1 fusion.33
  23.7 50.3 %shard_map.222 = f32[8,128,128]{2,1,0:T(8,128)} custom-call(f32[8,136,128]{2,1,0:T(8,128)} %pad_maximum_fusion.1.own_ref), custom_call_target="tpu_custom_call" | custom-call | tf_op jit(solution)/shard_map/pallas_call | solution.py:136
  74.1 1.6 convolution_bitcast_fusion.2
  75.7 1.4 fusion.6
  79.2 1.4 multiply_reduce_fusion.7
  81.3 7.8 %shard_map.224 = f32[40,128]{1,0:T(8,128)} custom-call(f32[40,128]{1,0:T(8,128)} %maximum_maximum_fusion.own_ref), custom_call_target="tpu_custom_call" | custom-call | tf_op jit(solution)/shard_map/pallas_call | solution.py:170
  90.6 2.5 %fusion.110 = (bf16[128,1024]{1,0:T(8,128)(2,1)}, f32[128,1024]{1,0:T(8,128)S(1)}, f32[16,8,8,128]{3,2,1,0:T(8,128)}, f32[128,1024]{1,0:T(8,128)S(1)}) fusion(f32[128,1024]{1,0:T(8,128)S(1)} %copy.54, f32[128]{0:T(128)S(1)} %fusion.98, bf16[128,1024]{1,0:T(8,128)(2,1)} %param.17, f32[128,1024]{1,0:T(8,128)} %get-tuple-element.365, ...), kind=kLoop, calls=%fused_computation.178 | loop fusion | flops 2490368 | bytes 3671040 | tf_op jit(solution)/shard_map/convert_element_type | solution.py:502
  95.2 1.6 convolution_bitcast_fusion.6
  98.4 45.9 %shard_map.225 = f32[8,128,128]{2,1,0:T(8,128)} custom-call(f32[8,136,128]{2,1,0:T(8,128)} %pad_maximum_fusion.own_ref), custom_call_target="tpu_custom_call" | custom-call | tf_op jit(solution)/shard_map/pallas_call | solution.py:136
  144.3 1.8 multiply_reduce_fusion.1
  148.9 1.3 fusion.45
  154.3 8.1 %shard_map.226 = f32[32,128]{1,0:T(8,128)} custom-call(f32[8,32,128]{2,1,0:T(8,128)} %pad_maximum_fusion.4.own_ref), custom_call_target="tpu_custom_call" | custom-call | tf_op jit(solution)/shard_map/pallas_call | solution.py:199
  162.4 1.3 fusion.116
  164.8 1.3 collective-permute-start.1
  168.4 2.1 collective-permute-done.1
  171.8 1.0 fusion.9.own_ref
  172.8 8.1 %shard_map.227 = f32[32,128]{1,0:T(8,128)} custom-call(f32[32,128]{1,0:T(8,128)} %fusion.9.own_ref), custom_call_target="tpu_custom_call" | custom-call | tf_op jit(solution)/shard_map/pallas_call | solution.py:170
  180.9 1.8 fusion.7
  186.8 1.0 reshape.268.own_ref
  187.8 42.8 %shard_map.228 = f32[8,8,16,128]{3,2,1,0:T(8,128)} custom-call(f32[8,8,16,128]{3,2,1,0:T(8,128)} %reshape.268.own_ref), custom_call_target="tpu_custom_call" | custom-call | tf_op jit(solution)/shard_map/pallas_call | solution.py:250
  230.6 1.2 reshape.269
  (160 shorter events, 34.0 us)
Async XLA Ops:
  0.6 8.7 %copy-start = (bf16[128,512]{1,0:T(8,128)(2,1)S(1)}, bf16[128,512]{1,0:T(8,128)(2,1)}, u32[]{:S(2)}) copy-start(bf16[128,512]{1,0:T(8,128)(2,1)} %param.15) | copy-start | bytes 393220
  0.7 5.1 %copy-start.38 = (f32[128,8]{0,1:T(8,128)S(1)}, f32[128,8]{0,1:T(8,128)}, u32[]{:S(2)}) copy-start(f32[128,8]{0,1:T(8,128)} %param.20) | copy-start | bytes 12292
  0.7 6.8 %copy-start.33 = (bf16[4,1024]{1,0:T(4,128)(2,1)S(1)}, bf16[4,1024]{1,0:T(4,128)(2,1)}, u32[]{:S(2)}) copy-start(bf16[4,1024]{1,0:T(4,128)(2,1)} %param.21) | copy-start | bytes 24580
  1.4 6.0 %copy-start.9 = (bf16[128,128]{1,0:T(8,128)(2,1)S(1)}, bf16[128,128]{1,0:T(8,128)(2,1)}, u32[]{:S(2)}) copy-start(bf16[128,128]{1,0:T(8,128)(2,1)} %param.19) | copy-start | bytes 98308
  1.4 19.5 %collective-permute-start = (bf16[3,1024]{1,0:T(4,128)(2,1)S(1)}, bf16[3,1024]{1,0:T(4,128)(2,1)S(1)}, u32[]{:S(2)}, u32[]{:S(2)}) collective-permute-start(bf16[3,1024]{1,0:T(4,128)(2,1)S(1)} %slice.97), channel_id=1, source_target_pairs={{0,8},{8,16},{16,24},{24,32},{32,40},{40,48},{48,56},{56,64},{64,7... | collective-permute-start | bytes 18440 | tf_op jit(solution)/shard_map/ppermute | solution.py:281
  7.5 13.5 %copy-start.27 = (f32[1,1024]{1,0:T(1,128)}, f32[1,1024]{1,0:T(1,128)S(1)}, u32[]{:S(2)}) copy-start(f32[1,1024]{1,0:T(1,128)S(1)} %get-tuple-element.358) | copy-start | bytes 12292
  7.5 13.5 %copy-start.29 = (f32[1,1024]{1,0:T(1,128)}, f32[1,1024]{1,0:T(1,128)S(1)}, u32[]{:S(2)}) copy-start(f32[1,1024]{1,0:T(1,128)S(1)} %get-tuple-element.359) | copy-start | bytes 12292
  7.5 13.5 %copy-start.31 = (f32[1,1024]{1,0:T(1,128)}, f32[1,1024]{1,0:T(1,128)S(1)}, u32[]{:S(2)}) copy-start(f32[1,1024]{1,0:T(1,128)S(1)} %get-tuple-element.360) | copy-start | bytes 12292
  10.7 65.0 %copy-start.18 = (pred[128,128]{1,0:T(8,128)(4,1)}, pred[128,128]{1,0:T(8,128)(4,1)S(1)}, u32[]{:S(2)}) copy-start(pred[128,128]{1,0:T(8,128)(4,1)S(1)} %iota_compare_fusion) | copy-start | bytes 49156
  19.8 1.1 copy-start.14
  78.1 12.5 %copy-start.5 = (f32[128,1024]{1,0:T(8,128)}, f32[128,1024]{1,0:T(8,128)S(1)}, u32[]{:S(2)}) copy-start(f32[128,1024]{1,0:T(8,128)S(1)} %copy.54) | copy-start | bytes 1572868
  78.1 1.2 copy-start.44
  94.1 1.1 copy-start.2
  144.3 1.8 copy-start.1
  147.1 1.0 copy-start.7
  152.6 11.3 %copy-start.8 = (f32[128,1024]{1,0:T(8,128)S(1)}, f32[128,1024]{1,0:T(8,128)}, u32[]{:S(2)}) copy-start(f32[128,1024]{1,0:T(8,128)} %get-tuple-element.347) | copy-start | bytes 1572868
  152.9 11.1 %copy-start.4 = (f32[128,1024]{1,0:T(8,128)S(1)}, f32[128,1024]{1,0:T(8,128)}, u32[]{:S(2)}) copy-start(f32[128,1024]{1,0:T(8,128)} %copy-done.3) | copy-start | bytes 1572868
  164.8 5.6 %collective-permute-start.1 = (f32[3,1024]{1,0:T(4,128)S(1)}, f32[3,1024]{1,0:T(4,128)S(1)}, u32[]{:S(2)}, u32[]{:S(2)}) collective-permute-start(f32[3,1024]{1,0:T(4,128)S(1)} %slice.134), channel_id=1, source_target_pairs={{8,0},{16,8},{24,16},{32,24},{40,32},{48,40},{56,48},{64,56},{72,6... | collective-permute-start | bytes 36872 | tf_op jit(solution)/shard_map/ppermute | solution.py:281
  167.5 2.9 %copy-start.28 = (f32[1,1024]{1,0:T(1,128)S(1)}, f32[1,1024]{1,0:T(1,128)}, u32[]{:S(2)}) copy-start(f32[1,1024]{1,0:T(1,128)} %copy-done.27) | copy-start | bytes 12292
  167.5 2.9 %copy-start.30 = (f32[1,1024]{1,0:T(1,128)S(1)}, f32[1,1024]{1,0:T(1,128)}, u32[]{:S(2)}) copy-start(f32[1,1024]{1,0:T(1,128)} %copy-done.29) | copy-start | bytes 12292
  167.5 2.9 %copy-start.32 = (f32[1,1024]{1,0:T(1,128)S(1)}, f32[1,1024]{1,0:T(1,128)}, u32[]{:S(2)}) copy-start(f32[1,1024]{1,0:T(1,128)} %copy-done.31) | copy-start | bytes 12292
  168.3 3.1 %copy-start.21 = (bf16[2,32,1024]{2,1,0:T(8,128)(2,1)S(1)}, bf16[2,32,1024]{2,1,0:T(8,128)(2,1)}, u32[]{:S(2)}) copy-start(bf16[2,32,1024]{2,1,0:T(8,128)(2,1)} %param.25) | copy-start | bytes 393220
  172.8 8.1 %copy-start.23 = (bf16[512,32]{0,1:T(8,128)(2,1)S(1)}, bf16[512,32]{0,1:T(8,128)(2,1)}, u32[]{:S(2)}) copy-start(bf16[512,32]{0,1:T(8,128)(2,1)} %param.24) | copy-start | bytes 98308
  180.9 1.8 copy-start.20
  (26 other events, 21.2 us)

commit v2 on v0

v2 whole, which is shorter than its diff:
```python
import jax
import jax.numpy as jnp
from jax import lax
from jax.experimental import pallas as pl
from jax.experimental.pallas import tpu as pltpu
from jax.sharding import PartitionSpec as P

ADAPTER_SCALE = 2.0
NORM_EPS = 1e-05
SIDE = 8
HDIM = 128
NSTATE = 128
TOK = 128
RANK = 32
KCONV = 4
SLICE = NSTATE // SIDE
OWN = TOK // SIDE
EARLY = 80
LATE = 48
MESH = pl.DeviceIdType.MESH
F32 = jnp.float32
BF16 = jnp.bfloat16


def own_place(kind):
    if kind == "head":
        return lax.axis_index("head")
    seq = lax.axis_index("seq")
    return lax.rem(seq, SIDE) if kind == "z" else seq // SIDE


def along(kind, step):
    if kind == "head":
        place = lax.rem(lax.axis_index("head") + step, SIDE)
        return {"head": place}, place
    seq = lax.axis_index("seq")
    if kind == "seq":
        place = lax.rem(seq + step + SIDE * SIDE, SIDE * SIDE)
        return {"seq": place}, place
    row, col = seq // SIDE, lax.rem(seq, SIDE)
    if kind == "z":
        place = lax.rem(col + step, SIDE)
        return {"seq": row * SIDE + place}, place
    place = lax.rem(row + step, SIDE)
    return {"seq": place * SIDE + col}, place


def send(device, source, target, send_sem, recv_sem):
    copy = pltpu.make_async_remote_copy(
        src_ref=source,
        dst_ref=target,
        send_sem=send_sem,
        recv_sem=recv_sem,
        device_id=device,
        device_id_type=MESH,
    )
    copy.start()
    return copy


class Copies:
    def __init__(self, send_sem, recv_sem):
        self.send_sem, self.recv_sem, self.used, self.all = send_sem, recv_sem, 0, []

    def start(self, device, source, target):
        at = self.used
        self.used += 1
        copy = send(device, source, target, self.send_sem.at[at], self.recv_sem.at[at])
        self.all.append(copy)
        return copy

    def exchange(self, kind, source, target):
        started = []
        for step in range(1, SIDE):
            device, place = along(kind, step)
            started.append(self.start(device, source(place), target))
        return started

    def left(self):
        for copy in self.all:
            copy.wait_send()


def arrived(copies):
    for copy in copies:
        copy.wait_recv()


def nn(a, b):
    return lax.dot_general(a, b, (((1,), (0,)), ((), ())), preferred_element_type=F32)


def nt(a, b):
    return lax.dot_general(a, b, (((1,), (1,)), ((), ())), preferred_element_type=F32)


def split(x):
    high = x.astype(BF16)
    return high, (x - high.astype(F32)).astype(BF16)


def left_exact(a, x, product=nn):
    high, low = split(x)
    return product(a, high) + product(a, low)


def right_exact(x, a, product=nn):
    high, low = split(x)
    return product(high, a) + product(low, a)


def both(x, y, product=nn):
    xh, xl = split(x)
    yh, yl = split(y)
    return product(xh, yh) + (product(xh, yl) + product(xl, yh))


def precise(a, b):
    return lax.dot_general(
        a, b, (((1,), (0,)), ((), ())), precision=lax.Precision.HIGHEST, preferred_element_type=F32
    )


def turned(x):
    missing = 128 - x.shape[1]
    if missing:
        x = jnp.concatenate([x, jnp.zeros((x.shape[0], missing), F32)], axis=1)
    return x.T


def sigmoid(x):
    return 1.0 / (1.0 + jnp.exp(-x))


def lanes(h):
    return pl.ds(pl.multiple_of(h * HDIM, HDIM), HDIM)


def each_head(step):
    lax.fori_loop(0, SIDE, lambda h, c: (step(h), c)[1], 0)


class Fold:
    def __init__(self, copies, refs, reverse):
        self.copies = copies
        (
            self.own, self.row_in, self.row_out, self.row_mix, self.part_out, self.part_in,
            self.enter_out, self.enter_in, self.out,
        ) = refs
        self.order = list(range(SIDE))[::-1] if reverse else list(range(SIDE))
        self.row, self.col = own_place("y"), own_place("z")

    def to_owner(self):
        self.flight = self.copies.exchange(
            "z", lambda place: self.own.at[place], self.row_in.at[self.col]
        )
        self.row_in[self.col] = self.own[self.col]

    def to_part(self):
        arrived(self.flight)
        state = jnp.zeros((NSTATE, HDIM), F32)
        total = jnp.zeros((8, HDIM), F32)
        for place in self.order:
            self.row_out[place] = state
            self.row_mix[place] = jnp.exp(total)
            step = self.row_in[place, NSTATE : NSTATE + 8]
            total = total + step
            state = jnp.exp(step[0:1]) * state + self.row_in[place, 0:NSTATE]
        for place in range(SIDE):
            self.part_out[place, 0:SLICE] = state[place * SLICE : (place + 1) * SLICE]
            self.part_out[place, SLICE : SLICE + 8] = total
        self.flight = self.copies.exchange(
            "y", lambda place: self.part_out.at[place], self.part_in.at[self.row]
        )
        self.part_in[self.row] = self.part_out[self.row]

    def to_row(self):
        arrived(self.flight)
        part = jnp.zeros((SLICE, HDIM), F32)
        for place in self.order:
            self.enter_out[place] = part
            decay = jnp.exp(self.part_in[place, SLICE : SLICE + 1])
            part = decay * part + self.part_in[place, 0:SLICE]
        self.flight = self.copies.exchange(
            "y", lambda place: self.enter_out.at[place], self.enter_in.at[self.row]
        )
        self.enter_in[self.row] = self.enter_out[self.row]

    def to_all(self):
        arrived(self.flight)
        enter = self.enter_in[...].reshape(NSTATE, HDIM)
        for place in range(SIDE):
            self.row_out[place] = self.row_out[place] + self.row_mix[place, 0:1] * enter
        self.flight = self.copies.exchange(
            "z", lambda place: self.row_out.at[place], self.out.at[self.col]
        )
        self.out[self.col] = self.row_out[self.col]

    def end(self):
        arrived(self.flight)


def fold_scratch():
    return [
        pltpu.VMEM((SIDE, NSTATE + 8, HDIM), F32),
        pltpu.VMEM((SIDE, NSTATE + 8, HDIM), F32),
        pltpu.VMEM((SIDE, NSTATE, HDIM), F32),
        pltpu.VMEM((SIDE, 8, HDIM), F32),
        pltpu.VMEM((SIDE, SLICE + 8, HDIM), F32),
        pltpu.VMEM((SIDE, SLICE + 8, HDIM), F32),
        pltpu.VMEM((SIDE, SLICE, HDIM), F32),
        pltpu.VMEM((SIDE, SLICE, HDIM), F32),
        pltpu.VMEM((SIDE, NSTATE, HDIM), F32),
    ]


class TokenSum:
    def __init__(self, copies, refs):
        self.copies = copies
        self.own, self.z_in, self.y_out, self.y_in, self.all = refs
        self.row, self.col = own_place("y"), own_place("z")

    def to_owner(self):
        self.flight = self.copies.exchange(
            "z", lambda place: self.own.at[place], self.z_in.at[self.col]
        )
        self.z_in[self.col] = self.own[self.col]

    def total(self, ref):
        total = ref[0]
        for place in range(1, SIDE):
            total = total + ref[place]
        return total

    def to_row(self):
        arrived(self.flight)
        self.y_out[...] = self.total(self.z_in)
        self.flight = self.copies.exchange("y", lambda place: self.y_out, self.y_in.at[self.row])
        self.y_in[self.row] = self.y_out[...]

    def to_all(self):
        arrived(self.flight)
        self.all[self.col] = self.total(self.y_in)
        self.flight = self.copies.exchange(
            "z", lambda place: self.all.at[self.col], self.all.at[self.col]
        )

    def end(self):
        arrived(self.flight)


def token_sum_scratch(rows):
    return [
        pltpu.VMEM((SIDE, rows, HDIM), F32),
        pltpu.VMEM((SIDE, rows, HDIM), F32),
        pltpu.VMEM((rows, HDIM), F32),
        pltpu.VMEM((SIDE, rows, HDIM), F32),
        pltpu.VMEM((SIDE, rows, HDIM), F32),
    ]


def head_total(ref):
    total = ref[0]
    for place in range(1, SIDE):
        total = total + ref[place]
    return total


COPIES = 2 + 4 * 7 + 2 * 4 * 7 + 2 * 3 * 7
WIDE = 13


def kernel(
    x_ref, conv_ref, gate_ref, b_ref, c_ref, l_ref, tap_ref, skip_ref, gain_ref, down_in_ref,
    up_in_ref, down_out_ref, up_out_ref, og_ref, base_ref,
    gconv_ref, ggate_ref, gb_ref, gc_ref, gl_ref, glayer_ref, ga_in_ref, gb_in_ref, ga_out_ref,
    gb_out_ref,
    *scratch,
):
    scratch = list(scratch)

    def take(n):
        out = scratch[:n]
        del scratch[:n]
        return out

    fold_refs, back_refs = take(9), take(9)
    early_refs, late_refs = take(5), take(5)
    (
        pre3, act3, slope3, y3, outer3, mix3, decay3, weighted3, gs3, dgs3, gssd3, ecum3, toend3,
    ) = take(WIDE)
    (cum_row, ext, halo, gext, halo_g, first_own, first_all, mid_own, mid_all, low_own, low_all,
     bc_own, bc_all, dcum3, gc_acc, gb_acc, dg_acc) = take(17)
    send_sem, recv_sem = take(2)

    seq, head = lax.axis_index("seq"), lax.axis_index("head")
    copies = Copies(send_sem, recv_sem)
    barrier = pltpu.get_barrier_semaphore()
    greeted = 0
    for kind, steps in (
        ("z", range(1, SIDE)), ("y", range(1, SIDE)), ("head", range(1, SIDE)), ("seq", (1, -1))
    ):
        for step in steps:
            pl.semaphore_signal(
                barrier, inc=1, device_id=along(kind, step)[0], device_id_type=MESH
            )
            greeted += 1

    first_own[0:RANK] = nt(up_out_ref[...], og_ref[...])
    first_own[RANK : 2 * RANK] = turned(nn(x_ref[...], down_in_ref[...]))[0:RANK]
    pl.semaphore_wait(barrier, greeted)
    tail = copies.start(along("seq", 1)[0], conv_ref.at[TOK - 16 : TOK], halo)
    first = copies.exchange("head", lambda place: first_own, first_all.at[head])
    first_all[head] = first_own[...]

    rows_at = lax.broadcasted_iota(jnp.int32, (TOK, TOK), 0)
    cols_at = lax.broadcasted_iota(jnp.int32, (TOK, TOK), 1)
    causal = rows_at >= cols_at
    cum = precise(causal.astype(F32), l_ref[...])
    cum_turned = turned(cum)[0:SIDE]
    cum_row[...] = cum_turned
    for h in range(SIDE):
        col = jnp.broadcast_to(cum[:, h : h + 1], (TOK, TOK))
        last = cum[TOK - 1 : TOK, h : h + 1]
        gap = col - cum_turned[h : h + 1]
        decay3[h] = jnp.where(causal, jnp.exp(jnp.where(causal, gap, 0.0)), 0.0)
        ecum3[h] = jnp.exp(col)
        toend3[h] = jnp.exp(jnp.broadcast_to(last, (TOK, TOK)) - col)
        total = jnp.broadcast_to(last, (8, HDIM))
        fold_refs[0][h, NSTATE : NSTATE + 8] = total
        back_refs[0][h, NSTATE : NSTATE + 8] = total
    b_turned = b_ref[...].astype(F32).T.astype(BF16)
    c_turned = c_ref[...].astype(F32).T.astype(BF16)
    scores = nt(c_ref[...], b_ref[...])
    scores_turned = nt(b_ref[...], c_ref[...])

    ext[8 : TOK + 8] = conv_ref[...].astype(F32)
    tail.wait_recv()
    before = halo[...].astype(F32)[8:16]
    ext[0:8] = jnp.where(seq > 0, before, 0.0)

    def local_state(h):
        at = lanes(h)
        taps = tap_ref[:, at].astype(F32)
        pre = ext[5 : 5 + TOK, at] * taps[0:1]
        for k in range(1, KCONV):
            pre = pre + ext[5 + k : 5 + k + TOK, at] * taps[k : k + 1]
        sig = sigmoid(pre)
        act = pre * sig
        act3[h] = act
        slope3[h] = sig * (1.0 + pre * (1.0 - sig))
        fold_refs[0][h, 0:NSTATE] = left_exact(b_turned, act * toend3[h])

    each_head(local_state)
    fold = Fold(copies, fold_refs, False)
    fold.to_owner()

    def inner(h):
        mix = decay3[h] * scores
        y3[h] = both(mix, act3[h]) + skip_ref[h] * act3[h]

    each_head(inner)
    fold.to_part()

    arrived(first)
    sums = head_total(first_all)
    back_out_turned = sums[0:RANK]
    low_in_turned = sums[RANK : 2 * RANK]
    back_out = turned(jnp.concatenate([back_out_turned, jnp.zeros((96, TOK), F32)], axis=0))[:, 0:RANK]

    def norm_gradient(h):
        at = lanes(h)
        down = down_out_ref[pl.ds(pl.multiple_of(h * HDIM, HDIM), HDIM), :]
        weighted3[h] = (
            base_ref[:, at].astype(F32) + ADAPTER_SCALE * right_exact(back_out, down, nt)
        ) * gain_ref[:, at]
        gate = gate_ref[:, at].astype(F32)
        sig = sigmoid(gate)
        gs3[h] = gate * sig
        dgs3[h] = sig * (1.0 + gate * (1.0 - sig))

    each_head(norm_gradient)
    fold.to_row()
    fold.to_all()
    fold.end()
    state_in = fold.out

    def gated_sums(h, carry):
        square, dot, low = carry
        at = lanes(h)
        outer = ecum3[h] * left_exact(c_ref[...], state_in[h])
        outer3[h] = outer
        y = y3[h] + outer
        y3[h] = y
        gated = y * gs3[h]
        down = down_out_ref[pl.ds(pl.multiple_of(h * HDIM, HDIM), HDIM), :]
        square = square + gated * gated
        dot = dot + weighted3[h] * gated
        low = low + right_exact(gated * gain_ref[:, at], down)
        return square, dot, low

    square, dot, low = lax.fori_loop(
        0, SIDE, gated_sums,
        (jnp.zeros((TOK, HDIM), F32), jnp.zeros((TOK, HDIM), F32), jnp.zeros((TOK, RANK), F32)),
    )
    mid_own[...] = turned(
        jnp.concatenate(
            [
                low,
                jnp.sum(square, axis=1, keepdims=True),
                jnp.sum(dot, axis=1, keepdims=True),
                jnp.zeros((TOK, 128 - RANK - 2), F32),
            ],
            axis=1,
        )
    )[0 : RANK + 8]
    mid = copies.exchange("head", lambda place: mid_own, mid_all.at[head])
    mid_all[head] = mid_own[...]
    arrived(mid)
    sums = head_total(mid_all)
    inv_row = lax.rsqrt(sums[RANK : RANK + 1] / (SIDE * SIDE * HDIM) + NORM_EPS)
    kappa_row = inv_row * inv_row * inv_row * sums[RANK + 1 : RANK + 2] / (SIDE * SIDE * HDIM)
    low_out_turned = sums[0:RANK] * inv_row
    columns = turned(jnp.concatenate([inv_row, kappa_row, jnp.zeros((126, TOK), F32)], axis=0))
    inv = jnp.broadcast_to(columns[:, 0:1], (TOK, HDIM))
    kappa = jnp.broadcast_to(columns[:, 1:2], (TOK, HDIM))

    def mixer_gradient(h):
        gated = y3[h] * gs3[h]
        grad_gated = inv * weighted3[h] - gated * kappa
        gssd = grad_gated * gs3[h]
        gssd3[h] = gssd
        pre3[h] = grad_gated * y3[h] * dgs3[h]
        back_refs[0][h, 0:NSTATE] = left_exact(c_turned, gssd * ecum3[h])

    each_head(mixer_gradient)
    back = Fold(copies, back_refs, True)
    back.to_owner()

    gc_acc[...] = jnp.zeros((TOK, NSTATE), F32)
    dg_acc[...] = jnp.zeros((TOK, TOK), F32)

    def local_gradient(h):
        gssd = gssd3[h]
        act = act3[h]
        decay = decay3[h]
        part = both(gssd, act, nt) * decay
        dg_acc[...] += part
        moved = part * scores
        away = turned(moved)
        dcum3[h] = moved - away + gssd * outer3[h]
        mix_turned = turned(decay) * scores_turned
        mix3[h] = both(mix_turned, gssd) + skip_ref[h] * gssd
        gc_acc[...] += both(gssd * ecum3[h], state_in[h], nt)

    each_head(local_gradient)
    back.to_part()

    scale = ADAPTER_SCALE / (SIDE * SIDE * TOK)
    early = TokenSum(copies, early_refs)

    def early_parts(h):
        at = lanes(h)
        ggate = pre3[h]
        ggate_ref[:, at] = ggate.astype(BF16)
        early.own[h, 0:RANK] = scale * both(low_in_turned, ggate)
        normed = y3[h] * gs3[h] * gain_ref[:, at] * inv
        early.own[h, RANK : 2 * RANK] = scale * both(back_out_turned, normed)

    each_head(early_parts)
    back.to_row()
    dg = dg_acc[...]
    gc_acc[...] += right_exact(dg, b_ref[...])
    gb_acc[...] = right_exact(turned(dg), c_ref[...])
    grad_b_out = scale * right_exact(low_out_turned, og_ref[...])
    for part in range(SIDE):
        early.own[part, 2 * RANK : 2 * RANK + 16] = grad_b_out[
            16 * (part % 2) : 16 * (part % 2) + 16, HDIM * (part // 2) : HDIM * (part // 2 + 1)
        ]
    back.to_all()
    early.to_owner()
    back.end()
    state_grad = back.out

    def state_gradient(h):
        toend = toend3[h]
        act = act3[h]
        into = toend * left_exact(b_ref[...], state_grad[h])
        gb_acc[...] += both(act * toend, state_grad[h], nt)
        fell = act * into
        total = jnp.sum(fell, axis=0, keepdims=True) + ecum3[h, TOK - 1 : TOK] * jnp.sum(
            state_in[h] * state_grad[h], axis=0, keepdims=True
        )
        dcum = dcum3[h] - fell
        dcum3[h] = jnp.where(rows_at == TOK - 1, dcum + total, dcum)
        gpre = (mix3[h] + into) * slope3[h]
        gext[0:TOK, lanes(h)] = gpre

    each_head(state_gradient)
    rim = copies.start(along("seq", -1)[0], gext.at[0:8], halo_g)
    for part in range(SIDE):
        bc_own[part, 0:OWN] = gb_acc[OWN * part : OWN * (part + 1)]
        bc_own[part, OWN : 2 * OWN] = gc_acc[OWN * part : OWN * (part + 1)]
    rows_out = copies.exchange("head", lambda place: bc_own.at[place], bc_all.at[head])
    bc_all[head] = bc_own[head]
    early.to_row()
    dcum = jnp.concatenate(
        [jnp.sum(dcum3[h], axis=1, keepdims=True) for h in range(SIDE)], axis=1
    )
    gl_ref[...] = precise((rows_at <= cols_at).astype(F32), dcum)
    rim.wait_recv()
    gext[TOK : TOK + 8] = jnp.where(seq < SIDE * SIDE - 1, halo_g[...], 0.0)
    late = TokenSum(copies, late_refs)

    def conv_gradient(h, low):
        at = lanes(h)
        taps = tap_ref[:, at].astype(F32)
        gconv = gext[3 : 3 + TOK, at] * taps[0:1]
        for k in range(1, KCONV):
            gconv = gconv + gext[3 - k : 3 - k + TOK, at] * taps[k : k + 1]
        gconv_ref[:, at] = gconv.astype(BF16)
        late.own[h, 0:RANK] = scale * both(low_in_turned, gconv)
        return low + (
            left_exact(up_in_ref[0, :, at], gconv, nt) + left_exact(up_in_ref[1, :, at], pre3[h], nt)
        )

    low_own[...] = lax.fori_loop(0, SIDE, conv_gradient, jnp.zeros((RANK, TOK), F32))
    low = copies.exchange("head", lambda place: low_own, low_all.at[head])
    low_all[head] = low_own[...]
    early.to_all()
    arrived(low)
    back_in_turned = head_total(low_all)
    grad_a_in = scale * right_exact(back_in_turned, x_ref[...])
    for part in range(SIDE):
        late.own[part, RANK : RANK + 16] = grad_a_in[
            16 * (part % 2) : 16 * (part % 2) + 16, HDIM * (part // 2) : HDIM * (part // 2 + 1)
        ]
    late.to_owner()
    back_in = turned(jnp.concatenate([back_in_turned, jnp.zeros((96, TOK), F32)], axis=0))[:, 0:RANK]
    glayer_ref[...] = (ADAPTER_SCALE * right_exact(back_in, down_in_ref[...], nt)).astype(BF16)
    arrived(rows_out)
    sums = head_total(bc_all)
    gb_ref[...] = sums[0:OWN]
    gc_ref[...] = sums[OWN : 2 * OWN]
    late.to_row()
    early.end()
    pad = jnp.zeros((96, HDIM), F32)
    for part in range(SIDE):
        at = slice(HDIM * part, HDIM * (part + 1))
        gb_in_ref[1, :, at] = early.all[part, 0:RANK]
        ga_out_ref[at, :] = turned(
            jnp.concatenate([early.all[part, RANK : 2 * RANK], pad], axis=0)
        )[:, 0:RANK]
        gb_out_ref[
            16 * (part % 2) : 16 * (part % 2) + 16, HDIM * (part // 2) : HDIM * (part // 2 + 1)
        ] = early.all[part, 2 * RANK : 2 * RANK + 16]
    late.to_all()
    late.end()
    for part in range(SIDE):
        gb_in_ref[0, :, HDIM * part : HDIM * (part + 1)] = late.all[part, 0:RANK]
    for part in range(SIDE // 2):
        ga_in_ref[HDIM * part : HDIM * (part + 1), :] = turned(
            jnp.concatenate(
                [
                    late.all[2 * part, RANK : RANK + 16],
                    late.all[2 * part + 1, RANK : RANK + 16],
                    pad,
                ],
                axis=0,
            )
        )[:, 0:RANK]
    copies.left()


def body(x, conv, gate, b, c, l, taps, skip, gain, down_in, up_in, down_out, up_out, og, base):
    outs = [
        jax.ShapeDtypeStruct(conv.shape, BF16),
        jax.ShapeDtypeStruct(gate.shape, BF16),
        jax.ShapeDtypeStruct((OWN, NSTATE), F32),
        jax.ShapeDtypeStruct((OWN, NSTATE), F32),
        jax.ShapeDtypeStruct(l.shape, F32),
        jax.ShapeDtypeStruct(x.shape, BF16),
        jax.ShapeDtypeStruct(down_in.shape, F32),
        jax.ShapeDtypeStruct(up_in.shape, F32),
        jax.ShapeDtypeStruct(down_out.shape, F32),
        jax.ShapeDtypeStruct(up_out.shape, F32),
    ]
    specs = [pl.BlockSpec(memory_space=pltpu.VMEM) for _ in range(15)]
    specs[7] = pl.BlockSpec(memory_space=pltpu.SMEM)
    wide = conv.shape[1]
    results = pl.pallas_call(
        kernel,
        out_shape=outs,
        in_specs=specs,
        out_specs=[pl.BlockSpec(memory_space=pltpu.VMEM) for _ in outs],
        scratch_shapes=fold_scratch()
        + fold_scratch()
        + token_sum_scratch(EARLY)
        + token_sum_scratch(LATE)
        + [pltpu.VMEM((SIDE, TOK, HDIM), F32) for _ in range(WIDE)]
        + [
            pltpu.VMEM((SIDE, TOK), F32),
            pltpu.VMEM((TOK + 8, wide), F32),
            pltpu.VMEM((16, wide), BF16),
            pltpu.VMEM((TOK + 8, wide), F32),
            pltpu.VMEM((8, wide), F32),
            pltpu.VMEM((2 * RANK, TOK), F32),
            pltpu.VMEM((SIDE, 2 * RANK, TOK), F32),
            pltpu.VMEM((RANK + 8, TOK), F32),
            pltpu.VMEM((SIDE, RANK + 8, TOK), F32),
            pltpu.VMEM((RANK, TOK), F32),
            pltpu.VMEM((SIDE, RANK, TOK), F32),
            pltpu.VMEM((SIDE, 2 * OWN, NSTATE), F32),
            pltpu.VMEM((SIDE, 2 * OWN, NSTATE), F32),
            pltpu.VMEM((SIDE, TOK, HDIM), F32),
            pltpu.VMEM((TOK, NSTATE), F32),
            pltpu.VMEM((TOK, NSTATE), F32),
            pltpu.VMEM((TOK, TOK), F32),
            pltpu.SemaphoreType.DMA((COPIES,)),
            pltpu.SemaphoreType.DMA((COPIES,)),
        ],
        compiler_params=pltpu.CompilerParams(
            collective_id=0, has_side_effects=True, vmem_limit_bytes=48 << 20
        ),
    )(
        x, conv, gate, b, c, l, taps, skip, gain.reshape(1, wide), down_in, up_in, down_out,
        up_out, og, base,
    )
    return tuple(results)


def solution(mesh):
    in_specs = (
        P("seq", "head"),
        P("seq", "head"),
        P("seq", "head"),
        P("seq", None),
        P("seq", None),
        P("seq", "head"),
        P(None, "head"),
        P("head"),
        P("head"),
        P("head", None),
        P(None, None, "head"),
        P("head", None),
        P(None, "head"),
        P("seq", "head"),
        P("seq", "head"),
    )
    out_specs = (
        P("seq", "head"),
        P("seq", "head"),
        P(("seq", "head"), None),
        P(("seq", "head"), None),
        P("seq", "head"),
        P("seq", "head"),
        P("head", None),
        P(None, None, "head"),
        P("head", None),
        P(None, "head"),
    )
    return jax.shard_map(body, mesh=mesh, in_specs=in_specs, out_specs=out_specs, check_vma=False)
```

time: 907 us -> 164 us (0.18)
  waiting for transfers between devices: 482 us -> 0 us
  blocking collectives: 206 us -> 0 us
  Pallas kernels: 0 us -> 147 us
  other arithmetic: 90.8 us -> 0 us
  local copies, waits for them, and re-layouts: 63.6 us -> 16.1 us
  matrix products: 35.3 us -> 0 us
  between operations: 14.8 us -> 0.74 us
    all_gather x2 -> x0, waiting for transfers between devices: 330 us -> none  [prefix(): gathered = jax.tree.map(lambda a: lax.all_gather(a, axis), part)]
    unnamed x1 -> x0, blocking collectives: 151 us -> none
    psum x1 -> x0, waiting for transfers between devices: 149 us -> none  [body(): lax.psum((averaging_scale * jnp.dot(layer_input_rows.astype(jnp.float32)....]
    pallas_call x0 -> x1, Pallas kernels: none -> 147 us  [body(): pl.pallas_call(kernel, out_shape=outs, in_specs=specs, out_specs=[pl.Bloc...]
    add x64 -> x0, other arithmetic: 74.8 us -> none  [the longest x63 74.8 us: chain_step(): jnp.exp(later_part[0])[:, None, None] * earlier[1] + later_part[1]]
    psum x3 -> x0, blocking collectives: 54.6 us -> none  [the longest x1 21.9 us: body(): reverse_in_grad = lax.psum(back_part, 'head')]
    exp x63 -> x0, local copies, waits for them, and re-layouts: 44 us -> none  [chain_step(): jnp.exp(later_part[0])[:, None, None] * earlier[1] + later_part[1]]
    dot_general x26 -> x0, matrix products: 35.3 us -> none  [the longest x3 5.66 us: advance(): jnp.einsum('hts,shp->thp', weights, x_block, precision=PRECISE_PRODUCT)]
  transfers between devices with their start and end apart: 7 -> 0, of which waited for: 4 -> 0; matrix products, arithmetic and copies ran while one was open for 18% -> 0% of each run, Pallas kernels for 0% -> 0%
where the time goes in v2:
time: 164 us
  Pallas kernels  147 us (90%)
  local copies, waits for them, and re-layouts  16.1 us (10%)
    pallas_call x1, Pallas kernels, body(): pl.pallas_call(kernel, out_shape=outs, in_specs=specs, out_specs=[pl.Bloc...  147 us
    unnamed x34, local copies, waits for them, and re-layouts  13.9 us

profile of v2, /device:TPU:6, one launch (start us, length us, event | category | flops | bytes accessed | tf_op | source)
XLA Modules:
  0.0 163.9 jit_solution(14563777714074388634)
XLA Ops:
  0.7 0.8 copy.25.l_ref
  1.5 0.9 copy.26.down_in_ref
  2.4 0.0 copy-start.6
  2.4 0.0 copy-start.10
  2.4 1.0 copy.27.down_out_ref
  3.5 0.9 copy-done.2
  4.5 0.9 copy-done.3
  5.4 0.9 copy-done.4
  6.3 0.9 copy-done.5
  7.2 0.8 copy-done.7
  7.9 0.8 copy-done.8
  8.7 0.7 copy-done.9
  9.4 0.7 copy-done.11
  10.0 147.0 %shard_map.222 = (bf16[128,1024]{1,0:T(8,128)(2,1)S(1)}, bf16[128,1024]{1,0:T(8,128)(2,1)S(1)}, f32[16,128]{1,0:T(8,128)S(1)}, f32[16,128]{1,0:T(8,128)S(1)}, f3...) custom-call(bf16[128,512]{1,0:T(8,128)(2,1)S(1)} %copy-done.3, ...), custom_call_target="tpu_custom_call" | custom-call | tf_op jit(solution)/shard_map/pallas_call | solution.py:591
  157.1 0.7 copy.28
  157.7 0.7 copy.29
  158.5 0.8 copy.30
  159.3 0.7 copy.38
  160.0 0.7 copy.39
  160.7 0.6 copy.40
  161.3 0.6 copy.41
  161.9 0.7 copy.42
  162.6 0.7 copy.43
  163.3 0.6 copy.44
  (14 shorter events, 0.0 us)
Async XLA Ops:
  0.6 2.8 %copy-start.1 = (bf16[128,1024]{1,0:T(8,128)(2,1)S(1)}, bf16[128,1024]{1,0:T(8,128)(2,1)}, u32[]{:S(2)}) copy-start(bf16[128,1024]{1,0:T(8,128)(2,1)} %gate_ref.1) | copy-start | bytes 786436
  1.5 2.0 %copy-start = (bf16[128,1024]{1,0:T(8,128)(2,1)S(1)}, bf16[128,1024]{1,0:T(8,128)(2,1)}, u32[]{:S(2)}) copy-start(bf16[128,1024]{1,0:T(8,128)(2,1)} %conv_ref.1) | copy-start | bytes 786436
  2.4 1.1 copy-start.6
  2.4 1.1 copy-start.10
  3.5 1.0 copy-start.2
  4.5 0.9 copy-start.3
  5.4 0.9 copy-start.4
  6.3 0.9 copy-start.5
  7.2 0.8 copy-start.7
  7.9 0.8 copy-start.8
  8.7 0.7 copy-start.9
  9.4 0.7 copy-start.11

commit v3 on v2

v3 whole, which is shorter than its diff:
```python
import jax
import jax.numpy as jnp
from jax import lax
from jax.experimental import pallas as pl
from jax.experimental.pallas import tpu as pltpu
from jax.sharding import PartitionSpec as P

ADAPTER_SCALE = 2.0
NORM_EPS = 1e-05
SIDE = 8
HDIM = 128
NSTATE = 128
TOK = 128
RANK = 32
KCONV = 4
OWN = TOK // SIDE
HALF = NSTATE // 2
SLICE = HALF // SIDE
EARLY = 80
MESH = pl.DeviceIdType.MESH
F32 = jnp.float32
BF16 = jnp.bfloat16


def own_place(kind):
    if kind == "head":
        return lax.axis_index("head")
    seq = lax.axis_index("seq")
    return lax.rem(seq, SIDE) if kind == "z" else seq // SIDE


def along(kind, step):
    if kind == "head":
        place = lax.rem(lax.axis_index("head") + step, SIDE)
        return {"head": place}, place
    seq = lax.axis_index("seq")
    if kind == "seq":
        place = lax.rem(seq + step + SIDE * SIDE, SIDE * SIDE)
        return {"seq": place}, place
    row, col = seq // SIDE, lax.rem(seq, SIDE)
    if kind == "z":
        place = lax.rem(col + step, SIDE)
        return {"seq": row * SIDE + place}, place
    place = lax.rem(row + step, SIDE)
    return {"seq": place * SIDE + col}, place


def send(device, source, target, send_sem, recv_sem):
    copy = pltpu.make_async_remote_copy(
        src_ref=source,
        dst_ref=target,
        send_sem=send_sem,
        recv_sem=recv_sem,
        device_id=device,
        device_id_type=MESH,
    )
    copy.start()
    return copy


class Copies:
    def __init__(self, send_sem, recv_sem):
        self.send_sem, self.recv_sem, self.used, self.all = send_sem, recv_sem, 0, []

    def start(self, device, source, target):
        at = self.used
        self.used += 1
        copy = send(device, source, target, self.send_sem.at[at], self.recv_sem.at[at])
        self.all.append(copy)
        return copy

    def exchange(self, kind, source, target):
        started = []
        for step in range(1, SIDE):
            device, place = along(kind, step)
            started.append(self.start(device, source(place), target))
        return started

    def left(self):
        for copy in self.all:
            copy.wait_send()


def arrived(copies):
    for copy in copies:
        copy.wait_recv()


def nn(a, b):
    return lax.dot_general(a, b, (((1,), (0,)), ((), ())), preferred_element_type=F32)


def nt(a, b):
    return lax.dot_general(a, b, (((1,), (1,)), ((), ())), preferred_element_type=F32)


def split(x):
    high = x.astype(BF16)
    return high, (x - high.astype(F32)).astype(BF16)


def left_exact(a, x, product=nn):
    high, low = split(x)
    return product(a, high) + product(a, low)


def right_exact(x, a, product=nn):
    high, low = split(x)
    return product(high, a) + product(low, a)


def both(x, y, product=nn):
    xh, xl = split(x)
    yh, yl = split(y)
    return product(xh, yh) + (product(xh, yl) + product(xl, yh))


def precise(a, b):
    return lax.dot_general(
        a, b, (((1,), (0,)), ((), ())), precision=lax.Precision.HIGHEST, preferred_element_type=F32
    )


def turned(x):
    missing = 128 - x.shape[1]
    if missing:
        x = jnp.concatenate([x, jnp.zeros((x.shape[0], missing), F32)], axis=1)
    return x.T


def sigmoid(x):
    return 1.0 / (1.0 + jnp.exp(-x))


def lanes(h):
    return pl.ds(pl.multiple_of(h * HDIM, HDIM), HDIM)


def each_head(step):
    lax.fori_loop(0, SIDE, lambda h, c: (step(h), c)[1], 0)


class Fold:
    def __init__(self, copies, refs, reverse):
        self.copies = copies
        (
            self.own, self.row_in, self.row_out, self.row_mix, self.part_out, self.part_in,
            self.enter_out, self.enter_in, self.out,
        ) = refs
        self.order = list(range(SIDE))[::-1] if reverse else list(range(SIDE))
        self.row, self.col = own_place("y"), own_place("z")
        self.flight = [None, None]

    def to_owner(self):
        for half, at in ((0, pl.ds(0, 8 + HALF)), (1, pl.ds(8 + HALF, HALF))):
            self.flight[half] = self.copies.exchange(
                "z", lambda place: self.own.at[place, at], self.row_in.at[self.col, at]
            )
        self.row_in[self.col] = self.own[self.col]

    def to_part(self, half):
        arrived(self.flight[half])
        state = jnp.zeros((HALF, HDIM), F32)
        total = jnp.zeros((8, HDIM), F32)
        for place in self.order:
            self.row_out[half, place] = state
            if half == 0:
                self.row_mix[place] = jnp.exp(total)
            step = self.row_in[place, 0:8]
            total = total + step
            state = (
                jnp.exp(step[0:1]) * state
                + self.row_in[place, 8 + HALF * half : 8 + HALF * (half + 1)]
            )
        for place in range(SIDE):
            self.part_out[half, place, 8 : 8 + SLICE] = state[place * SLICE : (place + 1) * SLICE]
            self.part_out[half, place, 0:8] = total
        self.flight[half] = self.copies.exchange(
            "y",
            lambda place: self.part_out.at[half, place],
            self.part_in.at[half, self.row],
        )
        self.part_in[half, self.row] = self.part_out[half, self.row]

    def to_row(self, half):
        arrived(self.flight[half])
        part = jnp.zeros((SLICE, HDIM), F32)
        for place in self.order:
            self.enter_out[half, place] = part
            decay = jnp.exp(self.part_in[half, place, 0:1])
            part = decay * part + self.part_in[half, place, 8 : 8 + SLICE]
        self.flight[half] = self.copies.exchange(
            "y",
            lambda place: self.enter_out.at[half, place],
            self.enter_in.at[half, self.row],
        )
        self.enter_in[half, self.row] = self.enter_out[half, self.row]

    def to_all(self, half):
        arrived(self.flight[half])
        enter = self.enter_in[half].reshape(HALF, HDIM)
        for place in range(SIDE):
            self.row_out[half, place] = (
                self.row_out[half, place] + self.row_mix[place, 0:1] * enter
            )
        at = pl.ds(HALF * half, HALF)
        self.flight[half] = self.copies.exchange(
            "z", lambda place: self.row_out.at[half, place], self.out.at[self.col, at]
        )
        self.out[self.col, at] = self.row_out[half, self.col]

    def end(self, half):
        arrived(self.flight[half])


def fold_scratch():
    return [
        pltpu.VMEM((SIDE, NSTATE + 8, HDIM), F32),
        pltpu.VMEM((SIDE, NSTATE + 8, HDIM), F32),
        pltpu.VMEM((2, SIDE, HALF, HDIM), F32),
        pltpu.VMEM((SIDE, 8, HDIM), F32),
        pltpu.VMEM((2, SIDE, SLICE + 8, HDIM), F32),
        pltpu.VMEM((2, SIDE, SLICE + 8, HDIM), F32),
        pltpu.VMEM((2, SIDE, SLICE, HDIM), F32),
        pltpu.VMEM((2, SIDE, SLICE, HDIM), F32),
        pltpu.VMEM((SIDE, NSTATE, HDIM), F32),
    ]


class TokenSum:
    def __init__(self, copies, refs, first, second):
        self.copies, self.first, self.second = copies, first, second
        self.own, self.first_in, self.second_out, self.second_in, self.all = refs
        self.part, self.other = own_place(first), own_place(second)

    def to_owner(self):
        self.flight = self.copies.exchange(
            self.first, lambda place: self.own.at[place], self.first_in.at[self.part]
        )
        self.first_in[self.part] = self.own[self.part]

    def to_line(self):
        arrived(self.flight)
        self.second_out[...] = head_total(self.first_in)
        self.flight = self.copies.exchange(
            self.second, lambda place: self.second_out, self.second_in.at[self.other]
        )
        self.second_in[self.other] = self.second_out[...]

    def to_all(self):
        arrived(self.flight)
        self.all[self.part] = head_total(self.second_in)
        self.flight = self.copies.exchange(
            self.first, lambda place: self.all.at[self.part], self.all.at[self.part]
        )

    def end(self):
        arrived(self.flight)


def token_sum_scratch(rows):
    return [
        pltpu.VMEM((SIDE, rows, HDIM), F32),
        pltpu.VMEM((SIDE, rows, HDIM), F32),
        pltpu.VMEM((rows, HDIM), F32),
        pltpu.VMEM((SIDE, rows, HDIM), F32),
        pltpu.VMEM((SIDE, rows, HDIM), F32),
    ]


def head_total(ref):
    total = ref[0]
    for place in range(1, SIDE):
        total = total + ref[place]
    return total


COPIES = 2 + 2 * 8 * 7 + 5 * 7 + 5 * 3 * 7
WIDE = 13
INPUTS = 14


def kernel(*refs):
    refs = list(refs)

    def take(n):
        out = refs[:n]
        del refs[:n]
        return out

    sources = take(INPUTS)
    (skip_ref,) = take(1)
    targets = take(10)
    places = take(INPUTS)
    (x_ref, conv_ref, gate_ref, b_ref, c_ref, l_ref, tap_ref, gain_ref, down_in_ref, up_in_ref,
     down_out_ref, up_out_ref, og_ref, base_ref) = places
    results = take(10)
    (gconv_ref, ggate_ref, gb_ref, gc_ref, gl_ref, glayer_ref, ga_in_ref, gb_in_ref, ga_out_ref,
     gb_out_ref) = results
    fold_refs, back_refs = take(9), take(9)
    early_refs = take(5)
    conv_refs, low_refs = (take(5), take(5)), (take(5), take(5))
    (
        pre3, act3, slope3, y3, outer3, mix3, decay3, weighted3, gs3, dgs3, gssd3, ecum3, toend3,
    ) = take(WIDE)
    (ext, halo, gext, halo_g, first_own, first_all, mid_own, mid_all, out_own, out_all, low_own,
     low_all, bc_own, bc_all, dcum3, gc_acc, gb_acc, dg_acc) = take(18)
    send_sem, recv_sem, load_sem, store_sem = take(4)

    loads = [
        pltpu.make_async_copy(source, place, load_sem.at[i])
        for i, (source, place) in enumerate(zip(sources, places))
    ]
    for load in loads:
        load.start()

    stores = []

    def store(*done):
        for ref in done:
            i = next(i for i, result in enumerate(results) if result is ref)
            copy = pltpu.make_async_copy(ref, targets[i], store_sem.at[i])
            copy.start()
            stores.append(copy)

    seq, head = lax.axis_index("seq"), lax.axis_index("head")
    copies = Copies(send_sem, recv_sem)
    barrier = pltpu.get_barrier_semaphore()
    greeted = 0
    for kind, steps in (
        ("z", range(1, SIDE)), ("y", range(1, SIDE)), ("head", range(1, SIDE)), ("seq", (1, -1))
    ):
        for step in steps:
            pl.semaphore_signal(
                barrier, inc=1, device_id=along(kind, step)[0], device_id_type=MESH
            )
            greeted += 1
    for load in loads:
        load.wait()

    first_own[0:RANK] = nt(up_out_ref[...], og_ref[...])
    first_own[RANK : 2 * RANK] = nt(down_in_ref[...], x_ref[...])
    ext[8 : TOK + 8] = conv_ref[...].astype(F32)

    rows_at = lax.broadcasted_iota(jnp.int32, (TOK, TOK), 0)
    cols_at = lax.broadcasted_iota(jnp.int32, (TOK, TOK), 1)
    causal = rows_at >= cols_at
    cum_turned = precise(l_ref[...], (rows_at <= cols_at).astype(F32))
    cum = turned(jnp.concatenate([cum_turned, jnp.zeros((TOK - SIDE, TOK), F32)], axis=0))
    for h in range(SIDE):
        col = jnp.broadcast_to(cum[:, h : h + 1], (TOK, TOK))
        last = cum[TOK - 1 : TOK, h : h + 1]
        gap = col - cum_turned[h : h + 1]
        decay3[h] = jnp.where(causal, jnp.exp(jnp.where(causal, gap, 0.0)), 0.0)
        ecum3[h] = jnp.exp(col)
        toend3[h] = jnp.exp(jnp.broadcast_to(last, (TOK, TOK)) - col)
        total = jnp.broadcast_to(last, (8, HDIM))
        fold_refs[0][h, 0:8] = total
        back_refs[0][h, 0:8] = total
    b_turned = b_ref[...].astype(F32).T.astype(BF16)
    c_turned = c_ref[...].astype(F32).T.astype(BF16)
    scores = nt(c_ref[...], b_ref[...])
    scores_turned = nt(b_ref[...], c_ref[...])

    pl.semaphore_wait(barrier, greeted)
    tail = copies.start(along("seq", 1)[0], conv_ref.at[TOK - 16 : TOK], halo)
    first = copies.exchange("head", lambda place: first_own, first_all.at[head])
    first_all[head] = first_own[...]

    def gates(h):
        gate = gate_ref[:, lanes(h)].astype(F32)
        sig = sigmoid(gate)
        gs3[h] = gate * sig
        dgs3[h] = sig * (1.0 + gate * (1.0 - sig))

    each_head(gates)

    tail.wait_recv()
    before = halo[...].astype(F32)[8:16]
    ext[0:8] = jnp.where(seq > 0, before, 0.0)

    def local_state(h):
        at = lanes(h)
        taps = tap_ref[:, at].astype(F32)
        pre = ext[5 : 5 + TOK, at] * taps[0:1]
        for k in range(1, KCONV):
            pre = pre + ext[5 + k : 5 + k + TOK, at] * taps[k : k + 1]
        sig = sigmoid(pre)
        act = pre * sig
        act3[h] = act
        slope3[h] = sig * (1.0 + pre * (1.0 - sig))
        fold_refs[0][h, 8 : 8 + NSTATE] = left_exact(b_turned, act * toend3[h])

    each_head(local_state)
    fold = Fold(copies, fold_refs, False)
    fold.to_owner()

    def inner(h):
        mix = decay3[h] * scores
        y3[h] = both(mix, act3[h]) + skip_ref[h] * act3[h]

    each_head(inner)
    fold.to_part(0)
    fold.to_part(1)

    arrived(first)
    sums = head_total(first_all)
    back_out_turned = sums[0:RANK]
    low_in_turned = sums[RANK : 2 * RANK]
    pad = jnp.zeros((TOK - RANK, TOK), F32)
    back_out = turned(jnp.concatenate([back_out_turned, pad], axis=0))[:, 0:RANK]

    def norm_gradient(h):
        at = lanes(h)
        weighted3[h] = (
            base_ref[:, at].astype(F32)
            + ADAPTER_SCALE * right_exact(back_out, down_out_ref[:, at])
        ) * gain_ref[:, at]

    each_head(norm_gradient)
    fold.to_row(0)
    fold.to_row(1)
    fold.to_all(0)
    fold.to_all(1)
    fold.end(0)
    fold.end(1)
    state_in = fold.out

    def gated_sums(h, carry):
        square, dot = carry
        outer = ecum3[h] * left_exact(c_ref[...], state_in[h])
        outer3[h] = outer
        y = y3[h] + outer
        y3[h] = y
        gated = y * gs3[h]
        return square + gated * gated, dot + weighted3[h] * gated

    square, dot = lax.fori_loop(
        0, SIDE, gated_sums, (jnp.zeros((TOK, HDIM), F32), jnp.zeros((TOK, HDIM), F32))
    )
    mid_own[...] = turned(
        jnp.concatenate(
            [
                jnp.sum(square, axis=1, keepdims=True),
                jnp.sum(dot, axis=1, keepdims=True),
                jnp.zeros((TOK, HDIM - 2), F32),
            ],
            axis=1,
        )
    )[0:8]
    mid = copies.exchange("head", lambda place: mid_own, mid_all.at[head])
    mid_all[head] = mid_own[...]

    def project(h, low):
        at = lanes(h)
        return low + left_exact(down_out_ref[:, at], y3[h] * gs3[h] * gain_ref[:, at], nt)

    out_own[...] = lax.fori_loop(0, SIDE, project, jnp.zeros((RANK, TOK), F32))
    out = copies.exchange("head", lambda place: out_own, out_all.at[head])
    out_all[head] = out_own[...]
    arrived(mid)
    sums = head_total(mid_all)
    inv_row = lax.rsqrt(sums[0:1] / (SIDE * SIDE * HDIM) + NORM_EPS)
    kappa_row = inv_row * inv_row * inv_row * sums[1:2] / (SIDE * SIDE * HDIM)
    columns = turned(
        jnp.concatenate([inv_row, kappa_row, jnp.zeros((TOK - 2, TOK), F32)], axis=0)
    )
    inv = jnp.broadcast_to(columns[:, 0:1], (TOK, HDIM))
    kappa = jnp.broadcast_to(columns[:, 1:2], (TOK, HDIM))

    def mixer_gradient(h):
        gated = y3[h] * gs3[h]
        grad_gated = inv * weighted3[h] - gated * kappa
        gssd = grad_gated * gs3[h]
        gssd3[h] = gssd
        pre3[h] = grad_gated * y3[h] * dgs3[h]
        back_refs[0][h, 8 : 8 + NSTATE] = left_exact(c_turned, gssd * ecum3[h])

    each_head(mixer_gradient)
    back = Fold(copies, back_refs, True)
    back.to_owner()

    scale = ADAPTER_SCALE / (SIDE * SIDE * TOK)
    early = TokenSum(copies, early_refs, "y", "z")

    def early_parts(h):
        at = lanes(h)
        ggate = pre3[h]
        ggate_ref[:, at] = ggate.astype(BF16)
        early.own[h, 0:RANK] = scale * both(low_in_turned, ggate)
        normed = y3[h] * gs3[h] * gain_ref[:, at] * inv
        early.own[h, RANK : 2 * RANK] = scale * both(back_out_turned, normed)

    each_head(early_parts)
    arrived(out)
    low_out_turned = head_total(out_all) * inv_row
    grad_b_out = scale * right_exact(low_out_turned, og_ref[...])
    for part in range(SIDE):
        early.own[part, 2 * RANK : 2 * RANK + 16] = grad_b_out[
            16 * (part % 2) : 16 * (part % 2) + 16, HDIM * (part // 2) : HDIM * (part // 2 + 1)
        ]
    store(ggate_ref)
    early.to_owner()

    gc_acc[...] = jnp.zeros((TOK, NSTATE), F32)
    dg_acc[...] = jnp.zeros((TOK, TOK), F32)

    def local_gradient(h):
        gssd = gssd3[h]
        decay = decay3[h]
        part = both(gssd, act3[h], nt) * decay
        dg_acc[...] += part
        moved = part * scores
        dcum3[h] = moved - turned(moved) + gssd * outer3[h]
        mix3[h] = both(turned(decay) * scores_turned, gssd) + skip_ref[h] * gssd
        gc_acc[...] += both(gssd * ecum3[h], state_in[h], nt)

    each_head(local_gradient)
    back.to_part(0)
    back.to_part(1)
    early.to_line()
    dg = dg_acc[...]
    gc_acc[...] += right_exact(dg, b_ref[...])
    gb_acc[...] = right_exact(turned(dg), c_ref[...])
    back.to_row(0)
    back.to_row(1)
    back.to_all(0)
    back.to_all(1)
    early.to_all()
    back.end(0)
    back.end(1)
    state_grad = back.out

    def state_gradient(h):
        toend = toend3[h]
        act = act3[h]
        into = toend * left_exact(b_ref[...], state_grad[h])
        gb_acc[...] += both(act * toend, state_grad[h], nt)
        fell = act * into
        total = jnp.sum(fell, axis=0, keepdims=True) + ecum3[h, TOK - 1 : TOK] * jnp.sum(
            state_in[h] * state_grad[h], axis=0, keepdims=True
        )
        dcum = dcum3[h] - fell
        dcum3[h] = jnp.where(rows_at == TOK - 1, dcum + total, dcum)
        gext[0:TOK, lanes(h)] = (mix3[h] + into) * slope3[h]

    each_head(state_gradient)
    rim = copies.start(along("seq", -1)[0], gext.at[0:8], halo_g)
    for part in range(SIDE):
        bc_own[part, 0:OWN] = gb_acc[OWN * part : OWN * (part + 1)]
        bc_own[part, OWN : 2 * OWN] = gc_acc[OWN * part : OWN * (part + 1)]
    dcum = turned(
        jnp.concatenate(
            [jnp.sum(dcum3[h], axis=1, keepdims=True) for h in range(SIDE)]
            + [jnp.zeros((TOK, HDIM - SIDE), F32)],
            axis=1,
        )
    )[0:SIDE]
    gl_ref[...] = precise(dcum, causal.astype(F32))
    early.end()
    for part in range(SIDE):
        at = slice(HDIM * part, HDIM * (part + 1))
        gb_in_ref[1, :, at] = early.all[part, 0:RANK]
        ga_out_ref[:, at] = early.all[part, RANK : 2 * RANK]
        gb_out_ref[
            16 * (part % 2) : 16 * (part % 2) + 16, HDIM * (part // 2) : HDIM * (part // 2 + 1)
        ] = early.all[part, 2 * RANK : 2 * RANK + 16]
    store(gl_ref, ga_out_ref, gb_out_ref)
    rim.wait_recv()
    gext[TOK : TOK + 8] = jnp.where(seq < SIDE * SIDE - 1, halo_g[...], 0.0)
    axes = (("z", "y"), ("y", "z"))
    conv_sums = [TokenSum(copies, refs, *axis) for refs, axis in zip(conv_refs, axes)]
    low_sums = [TokenSum(copies, refs, *axis) for refs, axis in zip(low_refs, axes)]

    def conv_gradient(h, low):
        at = lanes(h)
        taps = tap_ref[:, at].astype(F32)
        gconv = gext[3 : 3 + TOK, at] * taps[0:1]
        for k in range(1, KCONV):
            gconv = gconv + gext[3 - k : 3 - k + TOK, at] * taps[k : k + 1]
        gconv_ref[:, at] = gconv.astype(BF16)
        grad = scale * both(low_in_turned, gconv)
        conv_sums[0].own[h] = grad[0:16]
        conv_sums[1].own[h] = grad[16:32]
        return low + (
            left_exact(up_in_ref[0, :, at], gconv, nt) + left_exact(up_in_ref[1, :, at], pre3[h], nt)
        )

    low_own[...] = lax.fori_loop(0, SIDE, conv_gradient, jnp.zeros((RANK, TOK), F32))
    store(gconv_ref)
    low = copies.exchange("head", lambda place: low_own, low_all.at[head])
    low_all[head] = low_own[...]
    for sums in conv_sums:
        sums.to_owner()
    arrived(low)
    back_in_turned = head_total(low_all)
    grad_a_in = scale * right_exact(back_in_turned, x_ref[...])
    for part in range(SIDE):
        at = slice(HDIM * (part // 2), HDIM * (part // 2 + 1))
        for sums, first_row in zip(low_sums, (8 * (part % 2), 16 + 8 * (part % 2))):
            sums.own[part] = grad_a_in[first_row : first_row + 8, at]
    for sums in low_sums:
        sums.to_owner()
    rows_out = copies.exchange("head", lambda place: bc_own.at[place], bc_all.at[head])
    bc_all[head] = bc_own[head]
    back_in = turned(jnp.concatenate([back_in_turned, pad], axis=0))[:, 0:RANK]
    glayer_ref[...] = (ADAPTER_SCALE * right_exact(back_in, down_in_ref[...])).astype(BF16)
    for sums in conv_sums + low_sums:
        sums.to_line()
    arrived(rows_out)
    sums = head_total(bc_all)
    gb_ref[...] = sums[0:OWN]
    gc_ref[...] = sums[OWN : 2 * OWN]
    store(glayer_ref, gb_ref, gc_ref)
    for sums in conv_sums + low_sums:
        sums.to_all()
    for sums in conv_sums + low_sums:
        sums.end()
    for part in range(SIDE):
        at = slice(HDIM * part, HDIM * (part + 1))
        gb_in_ref[0, 0:16, at] = conv_sums[0].all[part]
        gb_in_ref[0, 16:32, at] = conv_sums[1].all[part]
        at = slice(HDIM * (part // 2), HDIM * (part // 2 + 1))
        for sums, first_row in zip(low_sums, (8 * (part % 2), 16 + 8 * (part % 2))):
            ga_in_ref[first_row : first_row + 8, at] = sums.all[part]
    store(gb_in_ref, ga_in_ref)
    copies.left()
    for copy in stores:
        copy.wait()


def hand_over(*refs):
    count = (len(refs) - 2) // 3
    sources, targets, places = refs[:count], refs[count : 2 * count], refs[2 * count : 3 * count]
    load_sem, store_sem = refs[-2:]
    loads = [
        pltpu.make_async_copy(sources[i], places[i], load_sem.at[i]) for i in range(count)
    ]
    stores = [
        pltpu.make_async_copy(places[i], targets[i], store_sem.at[i]) for i in range(count)
    ]
    for load in loads:
        load.start()
    for load, store in zip(loads, stores):
        load.wait()
        store.start()
    for store in stores:
        store.wait()


def body(x, conv, gate, b, c, l, taps, skip, gain, down_in, up_in, down_out, up_out, og, base):
    wide = conv.shape[1]
    inputs = (
        x, conv, gate, b, c, l.T, taps, gain.reshape(1, wide), down_in.T, up_in, down_out.T,
        up_out, og, base,
    )
    outs = [
        jax.ShapeDtypeStruct(conv.shape, BF16),
        jax.ShapeDtypeStruct(gate.shape, BF16),
        jax.ShapeDtypeStruct((OWN, NSTATE), F32),
        jax.ShapeDtypeStruct((OWN, NSTATE), F32),
        jax.ShapeDtypeStruct(l.shape[::-1], F32),
        jax.ShapeDtypeStruct(x.shape, BF16),
        jax.ShapeDtypeStruct(down_in.shape[::-1], F32),
        jax.ShapeDtypeStruct(up_in.shape, F32),
        jax.ShapeDtypeStruct(down_out.shape[::-1], F32),
        jax.ShapeDtypeStruct(up_out.shape, F32),
    ]
    in_place = [pl.BlockSpec(memory_space=pl.ANY) for _ in outs]
    results = pl.pallas_call(
        kernel,
        out_shape=outs,
        in_specs=[pl.BlockSpec(memory_space=pl.ANY) for _ in inputs]
        + [pl.BlockSpec(memory_space=pltpu.SMEM)],
        out_specs=in_place,
        scratch_shapes=[pltpu.VMEM(a.shape, a.dtype) for a in inputs]
        + [pltpu.VMEM(a.shape, a.dtype) for a in outs]
        + fold_scratch()
        + fold_scratch()
        + token_sum_scratch(EARLY)
        + token_sum_scratch(16)
        + token_sum_scratch(16)
        + token_sum_scratch(8)
        + token_sum_scratch(8)
        + [pltpu.VMEM((SIDE, TOK, HDIM), F32) for _ in range(WIDE)]
        + [
            pltpu.VMEM((TOK + 8, wide), F32),
            pltpu.VMEM((16, wide), BF16),
            pltpu.VMEM((TOK + 8, wide), F32),
            pltpu.VMEM((8, wide), F32),
            pltpu.VMEM((2 * RANK, TOK), F32),
            pltpu.VMEM((SIDE, 2 * RANK, TOK), F32),
            pltpu.VMEM((8, TOK), F32),
            pltpu.VMEM((SIDE, 8, TOK), F32),
            pltpu.VMEM((RANK, TOK), F32),
            pltpu.VMEM((SIDE, RANK, TOK), F32),
            pltpu.VMEM((RANK, TOK), F32),
            pltpu.VMEM((SIDE, RANK, TOK), F32),
            pltpu.VMEM((SIDE, 2 * OWN, NSTATE), F32),
            pltpu.VMEM((SIDE, 2 * OWN, NSTATE), F32),
            pltpu.VMEM((SIDE, TOK, HDIM), F32),
            pltpu.VMEM((TOK, NSTATE), F32),
            pltpu.VMEM((TOK, NSTATE), F32),
            pltpu.VMEM((TOK, TOK), F32),
            pltpu.SemaphoreType.DMA((COPIES,)),
            pltpu.SemaphoreType.DMA((COPIES,)),
            pltpu.SemaphoreType.DMA((INPUTS,)),
            pltpu.SemaphoreType.DMA((len(outs),)),
        ],
        compiler_params=pltpu.CompilerParams(
            collective_id=0, has_side_effects=True, vmem_limit_bytes=60 << 20
        ),
    )(*inputs, skip)
    results = pl.pallas_call(
        hand_over,
        out_shape=outs,
        in_specs=in_place,
        out_specs=in_place,
        scratch_shapes=[pltpu.VMEM(a.shape, a.dtype) for a in outs]
        + [pltpu.SemaphoreType.DMA((len(outs),)), pltpu.SemaphoreType.DMA((len(outs),))],
        compiler_params=pltpu.CompilerParams(vmem_limit_bytes=60 << 20),
    )(*results)
    turn = (4, 6, 8)
    return tuple(r.T if i in turn else r for i, r in enumerate(results))


def solution(mesh):
    in_specs = (
        P("seq", "head"),
        P("seq", "head"),
        P("seq", "head"),
        P("seq", None),
        P("seq", None),
        P("seq", "head"),
        P(None, "head"),
        P("head"),
        P("head"),
        P("head", None),
        P(None, None, "head"),
        P("head", None),
        P(None, "head"),
        P("seq", "head"),
        P("seq", "head"),
    )
    out_specs = (
        P("seq", "head"),
        P("seq", "head"),
        P(("seq", "head"), None),
        P(("seq", "head"), None),
        P("seq", "head"),
        P("seq", "head"),
        P("head", None),
        P(None, None, "head"),
        P("head", None),
        P(None, "head"),
    )
    return jax.shard_map(body, mesh=mesh, in_specs=in_specs, out_specs=out_specs, check_vma=False)
```

time: 164 us -> 131 us (0.80)
  Pallas kernels: 147 us -> 129 us
  local copies, waits for them, and re-layouts: 16.1 us -> 0 us
    pallas_call x1 -> x2, Pallas kernels: 147 us -> 129 us  [the longest x1 127 us: body(): pl.pallas_call(kernel, out_shape=outs, in_specs=[pl.BlockSpec(memory_spac...]
    unnamed x34 -> x0, local copies, waits for them, and re-layouts: 13.9 us -> none
    pallas_call x3 -> x0, local copies, waits for them, and re-layouts: 2.23 us -> none  [body(): pl.pallas_call(kernel, out_shape=outs, in_specs=specs, out_specs=[pl.Bloc...]
where the time goes in v3:
time: 131 us; the launch traced here: 130 us
  Pallas kernels  129 us (98%)
    pallas_call x1, Pallas kernels, body(): pl.pallas_call(kernel, out_shape=outs, in_specs=[pl.BlockSpec(memory_spac...  127 us

profile of v3, /device:TPU:6, one launch (start us, length us, event | category | flops | bytes accessed | tf_op | source)
XLA Modules:
  0.0 130.0 jit_solution(1867534551796914418)
XLA Ops:
  0.6 127.2 %shard_map.222 = (bf16[128,1024]{1,0:T(8,128)(2,1)}, bf16[128,1024]{1,0:T(8,128)(2,1)}, f32[16,128]{1,0:T(8,128)}, f32[16,128]{1,0:T(8,128)}, f32[8,128]{1,0:T(8...) custom-call(bf16[128,512]{1,0:T(8,128)(2,1)} %refs_0_.1, ...), custom_call_target="tpu_custom_call" | custom-call | tf_op jit(solution)/shard_map/pallas_call | solution.py:670
  127.8 2.1 %shard_map.223 = (bf16[128,1024]{1,0:T(8,128)(2,1)}, bf16[128,1024]{1,0:T(8,128)(2,1)}, f32[16,128]{1,0:T(8,128)}, f32[16,128]{1,0:T(8,128)}, f32[8,128]{1,0:T(8...) custom-call(bf16[128,1024]{1,0:T(8,128)(2,1)} %get-tuple-element.30., ...), custom_call_target="tpu_custom_call" | custom-call | tf_op jit(solution)/shard_map/pallas_call | solution.py:714

commit v4 on v3

--- a/solution.py
+++ b/solution.py
@@ -14,8 +14,8 @@
 RANK = 32
 KCONV = 4
 OWN = TOK // SIDE
-HALF = NSTATE // 2
-SLICE = HALF // SIDE
+CHUNKS = 4
+ROWS = NSTATE // CHUNKS
 EARLY = 80
 MESH = pl.DeviceIdType.MESH
 F32 = jnp.float32
@@ -145,84 +145,79 @@
         self.copies = copies
         (
             self.own, self.row_in, self.row_out, self.row_mix, self.part_out, self.part_in,
-            self.enter_out, self.enter_in, self.out,
+            self.out,
         ) = refs
         self.order = list(range(SIDE))[::-1] if reverse else list(range(SIDE))
         self.row, self.col = own_place("y"), own_place("z")
-        self.flight = [None, None]
-
-    def to_owner(self):
-        for half, at in ((0, pl.ds(0, 8 + HALF)), (1, pl.ds(8 + HALF, HALF))):
-            self.flight[half] = self.copies.exchange(
-                "z", lambda place: self.own.at[place, at], self.row_in.at[self.col, at]
-            )
-        self.row_in[self.col] = self.own[self.col]
-
-    def to_part(self, half):
-        arrived(self.flight[half])
-        state = jnp.zeros((HALF, HDIM), F32)
+        self.flight = [[] for _ in range(CHUNKS)]
+
+    def to_owner(self, chunk, step):
+        at = pl.ds(8 + ROWS * chunk, ROWS) if chunk else pl.ds(0, 8 + ROWS)
+        if step == SIDE:
+            self.row_in[self.col, at] = self.own[self.col, at]
+            return
+        device, place = along("z", step)
+        self.flight[chunk].append(
+            self.copies.start(device, self.own.at[place, at], self.row_in.at[self.col, at])
+        )
+
+    def to_column(self, chunk):
+        arrived(self.flight[chunk])
+        state = jnp.zeros((ROWS, HDIM), F32)
         total = jnp.zeros((8, HDIM), F32)
         for place in self.order:
-            self.row_out[half, place] = state
-            if half == 0:
+            self.row_out[chunk, place] = state
+            if chunk == 0:
                 self.row_mix[place] = jnp.exp(total)
             step = self.row_in[place, 0:8]
             total = total + step
             state = (
                 jnp.exp(step[0:1]) * state
-                + self.row_in[place, 8 + HALF * half : 8 + HALF * (half + 1)]
+                + self.row_in[place, 8 + ROWS * chunk : 8 + ROWS * (chunk + 1)]
             )
+        self.part_out[chunk, 0:8] = total
+        self.part_out[chunk, 8 : 8 + ROWS] = state
+        self.flight[chunk] = self.copies.exchange(
+            "y", lambda place: self.part_out.at[chunk], self.part_in.at[chunk, self.row]
+        )
+        self.part_in[chunk, self.row] = self.part_out[chunk]
+
+    def to_all(self, chunk):
+        arrived(self.flight[chunk])
+        part = jnp.zeros((ROWS, HDIM), F32)
+        enter = part
+        for place in self.order:
+            enter = jnp.where(self.row == place, part, enter)
+            decay = jnp.exp(self.part_in[chunk, place, 0:1])
+            part = decay * part + self.part_in[chunk, place, 8 : 8 + ROWS]
         for place in range(SIDE):
-            self.part_out[half, place, 8 : 8 + SLICE] = state[place * SLICE : (place + 1) * SLICE]
-            self.part_out[half, place, 0:8] = total
-        self.flight[half] = self.copies.exchange(
-            "y",
-            lambda place: self.part_out.at[half, place],
-            self.part_in.at[half, self.row],
-        )
-        self.part_in[half, self.row] = self.part_out[half, self.row]
-
-    def to_row(self, half):
-        arrived(self.flight[half])
-        part = jnp.zeros((SLICE, HDIM), F32)
-        for place in self.order:
-            self.enter_out[half, place] = part
-            decay = jnp.exp(self.part_in[half, place, 0:1])
-            part = decay * part + self.part_in[half, place, 8 : 8 + SLICE]
-        self.flight[half] = self.copies.exchange(
-            "y",
-            lambda place: self.enter_out.at[half, place],
-            self.enter_in.at[half, self.row],
-        )
-        self.enter_in[half, self.row] = self.enter_out[half, self.row]
-
-    def to_all(self, half):
-        arrived(self.flight[half])
-        enter = self.enter_in[half].reshape(HALF, HDIM)
-        for place in range(SIDE):
-            self.row_out[half, place] = (
-                self.row_out[half, place] + self.row_mix[place, 0:1] * enter
+            self.row_out[chunk, place] = (
+                self.row_out[chunk, place] + self.row_mix[place, 0:1] * enter
             )
-        at = pl.ds(HALF * half, HALF)
-        self.flight[half] = self.copies.exchange(
-            "z", lambda place: self.row_out.at[half, place], self.out.at[self.col, at]
-        )
-        self.out[self.col, at] = self.row_out[half, self.col]
-
-    def end(self, half):
-        arrived(self.flight[half])
+        at = pl.ds(ROWS * chunk, ROWS)
+        self.flight[chunk] = self.copies.exchange(
+            "z", lambda place: self.row_out.at[chunk, place], self.out.at[self.col, at]
+        )
+        self.out[self.col, at] = self.row_out[chunk, self.col]
+
+    def end(self, step):
+        for flight in self.flight:
+            if step:
+                flight[step - 1].wait_recv()
+        return lax.rem(self.col - step + SIDE, SIDE)
+
+
+NEAREST = (0, 1, 7, 2, 6, 3, 5, 4)
 
 
 def fold_scratch():
     return [
         pltpu.VMEM((SIDE, NSTATE + 8, HDIM), F32),
         pltpu.VMEM((SIDE, NSTATE + 8, HDIM), F32),
-        pltpu.VMEM((2, SIDE, HALF, HDIM), F32),
+        pltpu.VMEM((CHUNKS, SIDE, ROWS, HDIM), F32),
         pltpu.VMEM((SIDE, 8, HDIM), F32),
-        pltpu.VMEM((2, SIDE, SLICE + 8, HDIM), F32),
-        pltpu.VMEM((2, SIDE, SLICE + 8, HDIM), F32),
-        pltpu.VMEM((2, SIDE, SLICE, HDIM), F32),
-        pltpu.VMEM((2, SIDE, SLICE, HDIM), F32),
+        pltpu.VMEM((CHUNKS, ROWS + 8, HDIM), F32),
+        pltpu.VMEM((CHUNKS, SIDE, ROWS + 8, HDIM), F32),
         pltpu.VMEM((SIDE, NSTATE, HDIM), F32),
     ]
 
@@ -275,9 +270,10 @@
     return total
 
 
-COPIES = 2 + 2 * 8 * 7 + 5 * 7 + 5 * 3 * 7
+COPIES = 2 + 2 * 3 * CHUNKS * 7 + 5 * 7 + 5 * 3 * 7
 WIDE = 13
 INPUTS = 14
+FETCH_ORDER = (1, 5, 3, 6, 11, 12, 8, 0, 4, 2, 13, 10, 7, 9)
 
 
 def kernel(*refs):
@@ -297,22 +293,15 @@
     results = take(10)
     (gconv_ref, ggate_ref, gb_ref, gc_ref, gl_ref, glayer_ref, ga_in_ref, gb_in_ref, ga_out_ref,
      gb_out_ref) = results
-    fold_refs, back_refs = take(9), take(9)
+    fold_refs, back_refs = take(7), take(7)
     early_refs = take(5)
     conv_refs, low_refs = (take(5), take(5)), (take(5), take(5))
     (
         pre3, act3, slope3, y3, outer3, mix3, decay3, weighted3, gs3, dgs3, gssd3, ecum3, toend3,
     ) = take(WIDE)
     (ext, halo, gext, halo_g, first_own, first_all, mid_own, mid_all, out_own, out_all, low_own,
-     low_all, bc_own, bc_all, dcum3, gc_acc, gb_acc, dg_acc) = take(18)
+     low_all, bc_own, bc_all, dcum3, gc_acc, gb_acc, dg_acc, rim_own) = take(19)
     send_sem, recv_sem, load_sem, store_sem = take(4)
-
-    loads = [
-        pltpu.make_async_copy(source, place, load_sem.at[i])
-        for i, (source, place) in enumerate(zip(sources, places))
-    ]
-    for load in loads:
-        load.start()
 
     stores = []
 
@@ -328,56 +317,43 @@
     barrier = pltpu.get_barrier_semaphore()
     greeted = 0
     for kind, steps in (
-        ("z", range(1, SIDE)), ("y", range(1, SIDE)), ("head", range(1, SIDE)), ("seq", (1, -1))
+        ("seq", (1, -1)), ("z", range(1, SIDE)), ("y", range(1, SIDE)), ("head", range(1, SIDE))
     ):
         for step in steps:
             pl.semaphore_signal(
                 barrier, inc=1, device_id=along(kind, step)[0], device_id_type=MESH
             )
             greeted += 1
-    for load in loads:
-        load.wait()
-
-    first_own[0:RANK] = nt(up_out_ref[...], og_ref[...])
-    first_own[RANK : 2 * RANK] = nt(down_in_ref[...], x_ref[...])
+    loads = {}
+    for i in FETCH_ORDER:
+        loads[i] = pltpu.make_async_copy(sources[i], places[i], load_sem.at[i])
+        loads[i].start()
+
+    def fetched(*which):
+        for ref in which:
+            loads[next(i for i, place in enumerate(places) if place is ref)].wait()
+
+    fetched(conv_ref)
+    pl.semaphore_wait(barrier, greeted)
+    tail = copies.start(along("seq", 1)[0], conv_ref.at[TOK - 16 : TOK], halo)
     ext[8 : TOK + 8] = conv_ref[...].astype(F32)
-
     rows_at = lax.broadcasted_iota(jnp.int32, (TOK, TOK), 0)
     cols_at = lax.broadcasted_iota(jnp.int32, (TOK, TOK), 1)
     causal = rows_at >= cols_at
+    fetched(l_ref, b_ref, tap_ref)
     cum_turned = precise(l_ref[...], (rows_at <= cols_at).astype(F32))
     cum = turned(jnp.concatenate([cum_turned, jnp.zeros((TOK - SIDE, TOK), F32)], axis=0))
     for h in range(SIDE):
-        col = jnp.broadcast_to(cum[:, h : h + 1], (TOK, TOK))
         last = cum[TOK - 1 : TOK, h : h + 1]
-        gap = col - cum_turned[h : h + 1]
-        decay3[h] = jnp.where(causal, jnp.exp(jnp.where(causal, gap, 0.0)), 0.0)
-        ecum3[h] = jnp.exp(col)
-        toend3[h] = jnp.exp(jnp.broadcast_to(last, (TOK, TOK)) - col)
+        toend3[h] = jnp.exp(jnp.broadcast_to(last - cum[:, h : h + 1], (TOK, TOK)))
         total = jnp.broadcast_to(last, (8, HDIM))
         fold_refs[0][h, 0:8] = total
         back_refs[0][h, 0:8] = total
     b_turned = b_ref[...].astype(F32).T.astype(BF16)
-    c_turned = c_ref[...].astype(F32).T.astype(BF16)
-    scores = nt(c_ref[...], b_ref[...])
-    scores_turned = nt(b_ref[...], c_ref[...])
-
-    pl.semaphore_wait(barrier, greeted)
-    tail = copies.start(along("seq", 1)[0], conv_ref.at[TOK - 16 : TOK], halo)
-    first = copies.exchange("head", lambda place: first_own, first_all.at[head])
-    first_all[head] = first_own[...]
-
-    def gates(h):
-        gate = gate_ref[:, lanes(h)].astype(F32)
-        sig = sigmoid(gate)
-        gs3[h] = gate * sig
-        dgs3[h] = sig * (1.0 + gate * (1.0 - sig))
-
-    each_head(gates)
-
     tail.wait_recv()
     before = halo[...].astype(F32)[8:16]
     ext[0:8] = jnp.where(seq > 0, before, 0.0)
+    fold = Fold(copies, fold_refs, False)
 
     def local_state(h):
         at = lanes(h)
@@ -389,21 +365,45 @@
         act = pre * sig
         act3[h] = act
         slope3[h] = sig * (1.0 + pre * (1.0 - sig))
-        fold_refs[0][h, 8 : 8 + NSTATE] = left_exact(b_turned, act * toend3[h])
-
-    each_head(local_state)
-    fold = Fold(copies, fold_refs, False)
-    fold.to_owner()
+        fold.own[h, 8 : 8 + NSTATE] = left_exact(b_turned, act * toend3[h])
+
+    for step in range(1, SIDE + 1):
+        local_state(lax.rem(fold.col + step, SIDE))
+        fold.to_owner(0, step)
+    for chunk in range(1, CHUNKS):
+        for step in range(1, SIDE + 1):
+            fold.to_owner(chunk, step)
+
+    fetched(up_out_ref, og_ref, down_in_ref, x_ref)
+    first_own[0:RANK] = nt(up_out_ref[...], og_ref[...])
+    first_own[RANK : 2 * RANK] = nt(down_in_ref[...], x_ref[...])
+    first = copies.exchange("head", lambda place: first_own, first_all.at[head])
+    first_all[head] = first_own[...]
+
+    for h in range(SIDE):
+        col = jnp.broadcast_to(cum[:, h : h + 1], (TOK, TOK))
+        gap = col - cum_turned[h : h + 1]
+        decay3[h] = jnp.where(causal, jnp.exp(jnp.where(causal, gap, 0.0)), 0.0)
+        ecum3[h] = jnp.exp(col)
+    fetched(c_ref, gate_ref)
+    c_turned = c_ref[...].astype(F32).T.astype(BF16)
+    scores = nt(c_ref[...], b_ref[...])
+    scores_turned = nt(b_ref[...], c_ref[...])
 
     def inner(h):
         mix = decay3[h] * scores
         y3[h] = both(mix, act3[h]) + skip_ref[h] * act3[h]
-
+        gate = gate_ref[:, lanes(h)].astype(F32)
+        sig = sigmoid(gate)
+        gs3[h] = gate * sig
+        dgs3[h] = sig * (1.0 + gate * (1.0 - sig))
+
+    fold.to_column(0)
     each_head(inner)
-    fold.to_part(0)
-    fold.to_part(1)
+    fold.to_column(1)
 
     arrived(first)
+    fetched(base_ref, down_out_ref, gain_ref, up_in_ref)
     sums = head_total(first_all)
     back_out_turned = sums[0:RANK]
     low_in_turned = sums[RANK : 2 * RANK]
@@ -418,26 +418,22 @@
         ) * gain_ref[:, at]
 
     each_head(norm_gradient)
-    fold.to_row(0)
-    fold.to_row(1)
-    fold.to_all(0)
-    fold.to_all(1)
-    fold.end(0)
-    fold.end(1)
+    for chunk in range(2, CHUNKS):
+        fold.to_column(chunk)
+    for chunk in range(CHUNKS):
+        fold.to_all(chunk)
     state_in = fold.out
 
-    def gated_sums(h, carry):
-        square, dot = carry
+    square, dot = jnp.zeros((TOK, HDIM), F32), jnp.zeros((TOK, HDIM), F32)
+    for step in NEAREST:
+        h = fold.end(step)
         outer = ecum3[h] * left_exact(c_ref[...], state_in[h])
         outer3[h] = outer
         y = y3[h] + outer
         y3[h] = y
         gated = y * gs3[h]
-        return square + gated * gated, dot + weighted3[h] * gated
-
-    square, dot = lax.fori_loop(
-        0, SIDE, gated_sums, (jnp.zeros((TOK, HDIM), F32), jnp.zeros((TOK, HDIM), F32))
-    )
+        square = square + gated * gated
+        dot = dot + weighted3[h] * gated
     mid_own[...] = turned(
         jnp.concatenate(
             [
@@ -474,24 +470,29 @@
         gssd = grad_gated * gs3[h]
         gssd3[h] = gssd
         pre3[h] = grad_gated * y3[h] * dgs3[h]
-        back_refs[0][h, 8 : 8 + NSTATE] = left_exact(c_turned, gssd * ecum3[h])
-
-    each_head(mixer_gradient)
+        back.own[h, 8 : 8 + NSTATE] = left_exact(c_turned, gssd * ecum3[h])
+
     back = Fold(copies, back_refs, True)
-    back.to_owner()
+    for step in range(1, SIDE + 1):
+        mixer_gradient(lax.rem(back.col + step, SIDE))
+        back.to_owner(0, step)
+    for chunk in range(1, CHUNKS):
+        for step in range(1, SIDE + 1):
+            back.to_owner(chunk, step)
 
     scale = ADAPTER_SCALE / (SIDE * SIDE * TOK)
-    early = TokenSum(copies, early_refs, "y", "z")
-
-    def early_parts(h):
+    early = TokenSum(copies, early_refs, "z", "y")
+
+    def early_parts(h, low):
         at = lanes(h)
         ggate = pre3[h]
         ggate_ref[:, at] = ggate.astype(BF16)
         early.own[h, 0:RANK] = scale * both(low_in_turned, ggate)
         normed = y3[h] * gs3[h] * gain_ref[:, at] * inv
         early.own[h, RANK : 2 * RANK] = scale * both(back_out_turned, normed)
-
-    each_head(early_parts)
+        return low + left_exact(up_in_ref[1, :, at], ggate, nt)
+
+    low_gate = lax.fori_loop(0, SIDE, early_parts, jnp.zeros((RANK, TOK), F32))
     arrived(out)
     low_out_turned = head_total(out_all) * inv_row
     grad_b_out = scale * right_exact(low_out_turned, og_ref[...])
@@ -515,21 +516,25 @@
         mix3[h] = both(turned(decay) * scores_turned, gssd) + skip_ref[h] * gssd
         gc_acc[...] += both(gssd * ecum3[h], state_in[h], nt)
 
-    each_head(local_gradient)
-    back.to_part(0)
-    back.to_part(1)
-    early.to_line()
+    lax.fori_loop(0, SIDE // 2, lambda h, c: (local_gradient(h), c)[1], 0)
+    back.to_column(0)
+    lax.fori_loop(SIDE // 2, SIDE, lambda h, c: (local_gradient(h), c)[1], 0)
+    for chunk in range(1, CHUNKS):
+        back.to_column(chunk)
     dg = dg_acc[...]
     gc_acc[...] += right_exact(dg, b_ref[...])
     gb_acc[...] = right_exact(turned(dg), c_ref[...])
-    back.to_row(0)
-    back.to_row(1)
-    back.to_all(0)
-    back.to_all(1)
-    early.to_all()
-    back.end(0)
-    back.end(1)
+    for chunk in range(CHUNKS - 1):
+        back.to_all(chunk)
+    back.to_all(CHUNKS - 1)
+    early.to_line()
     state_grad = back.out
+
+    for step in NEAREST:
+        h = back.end(step)
+        into = toend3[h, 0:8] * left_exact(b_ref[0:16], state_grad[h])[0:8]
+        rim_own[:, lanes(h)] = (mix3[h, 0:8] + into) * slope3[h, 0:8]
+    rim = copies.start(along("seq", -1)[0], rim_own, halo_g)
 
     def state_gradient(h):
         toend = toend3[h]
@@ -545,27 +550,7 @@
         gext[0:TOK, lanes(h)] = (mix3[h] + into) * slope3[h]
 
     each_head(state_gradient)
-    rim = copies.start(along("seq", -1)[0], gext.at[0:8], halo_g)
-    for part in range(SIDE):
-        bc_own[part, 0:OWN] = gb_acc[OWN * part : OWN * (part + 1)]
-        bc_own[part, OWN : 2 * OWN] = gc_acc[OWN * part : OWN * (part + 1)]
-    dcum = turned(
-        jnp.concatenate(
-            [jnp.sum(dcum3[h], axis=1, keepdims=True) for h in range(SIDE)]
-            + [jnp.zeros((TOK, HDIM - SIDE), F32)],
-            axis=1,
-        )
-    )[0:SIDE]
-    gl_ref[...] = precise(dcum, causal.astype(F32))
-    early.end()
-    for part in range(SIDE):
-        at = slice(HDIM * part, HDIM * (part + 1))
-        gb_in_ref[1, :, at] = early.all[part, 0:RANK]
-        ga_out_ref[:, at] = early.all[part, RANK : 2 * RANK]
-        gb_out_ref[
-            16 * (part % 2) : 16 * (part % 2) + 16, HDIM * (part // 2) : HDIM * (part // 2 + 1)
-        ] = early.all[part, 2 * RANK : 2 * RANK + 16]
-    store(gl_ref, ga_out_ref, gb_out_ref)
+    early.to_all()
     rim.wait_recv()
     gext[TOK : TOK + 8] = jnp.where(seq < SIDE * SIDE - 1, halo_g[...], 0.0)
     axes = (("z", "y"), ("y", "z"))
@@ -579,19 +564,31 @@
         for k in range(1, KCONV):
             gconv = gconv + gext[3 - k : 3 - k + TOK, at] * taps[k : k + 1]
         gconv_ref[:, at] = gconv.astype(BF16)
-        grad = scale * both(low_in_turned, gconv)
+        y3[h] = gconv
+        return low + left_exact(up_in_ref[0, :, at], gconv, nt)
+
+    low_own[...] = lax.fori_loop(0, SIDE, conv_gradient, low_gate)
+    low = copies.exchange("head", lambda place: low_own, low_all.at[head])
+    low_all[head] = low_own[...]
+
+    def conv_parts(h):
+        grad = scale * both(low_in_turned, y3[h])
         conv_sums[0].own[h] = grad[0:16]
         conv_sums[1].own[h] = grad[16:32]
-        return low + (
-            left_exact(up_in_ref[0, :, at], gconv, nt) + left_exact(up_in_ref[1, :, at], pre3[h], nt)
-        )
-
-    low_own[...] = lax.fori_loop(0, SIDE, conv_gradient, jnp.zeros((RANK, TOK), F32))
-    store(gconv_ref)
-    low = copies.exchange("head", lambda place: low_own, low_all.at[head])
-    low_all[head] = low_own[...]
+
+    each_head(conv_parts)
     for sums in conv_sums:
         sums.to_owner()
+    store(gconv_ref)
+    dcum = turned(
+        jnp.concatenate(
+            [jnp.sum(dcum3[h], axis=1, keepdims=True) for h in range(SIDE)]
+            + [jnp.zeros((TOK, HDIM - SIDE), F32)],
+            axis=1,
+        )
+    )[0:SIDE]
+    gl_ref[...] = precise(dcum, causal.astype(F32))
+    store(gl_ref)
     arrived(low)
     back_in_turned = head_total(low_all)
     grad_a_in = scale * right_exact(back_in_turned, x_ref[...])
@@ -601,12 +598,24 @@
             sums.own[part] = grad_a_in[first_row : first_row + 8, at]
     for sums in low_sums:
         sums.to_owner()
+    for part in range(SIDE):
+        bc_own[part, 0:OWN] = gb_acc[OWN * part : OWN * (part + 1)]
+        bc_own[part, OWN : 2 * OWN] = gc_acc[OWN * part : OWN * (part + 1)]
     rows_out = copies.exchange("head", lambda place: bc_own.at[place], bc_all.at[head])
     bc_all[head] = bc_own[head]
     back_in = turned(jnp.concatenate([back_in_turned, pad], axis=0))[:, 0:RANK]
     glayer_ref[...] = (ADAPTER_SCALE * right_exact(back_in, down_in_ref[...])).astype(BF16)
     for sums in conv_sums + low_sums:
         sums.to_line()
+    early.end()
+    for part in range(SIDE):
+        at = slice(HDIM * part, HDIM * (part + 1))
+        gb_in_ref[1, :, at] = early.all[part, 0:RANK]
+        ga_out_ref[:, at] = early.all[part, RANK : 2 * RANK]
+        gb_out_ref[
+            16 * (part % 2) : 16 * (part % 2) + 16, HDIM * (part // 2) : HDIM * (part // 2 + 1)
+        ] = early.all[part, 2 * RANK : 2 * RANK + 16]
+    store(ga_out_ref, gb_out_ref)
     arrived(rows_out)
     sums = head_total(bc_all)
     gb_ref[...] = sums[0:OWN]
@@ -702,6 +711,7 @@
             pltpu.VMEM((TOK, NSTATE), F32),
             pltpu.VMEM((TOK, NSTATE), F32),
             pltpu.VMEM((TOK, TOK), F32),
+            pltpu.VMEM((8, wide), F32),
             pltpu.SemaphoreType.DMA((COPIES,)),
             pltpu.SemaphoreType.DMA((COPIES,)),
             pltpu.SemaphoreType.DMA((INPUTS,)),

time: 131 us -> 120 us (0.916)
  Pallas kernels: 129 us -> 119 us
    pallas_call x1, Pallas kernels: 127 us -> 117 us  [body(): pl.pallas_call(kernel, out_shape=outs, in_specs=[pl.BlockSpec(memory_spac...]
where the time goes in v4:
time: 120 us
  Pallas kernels  119 us (99%)
    pallas_call x1, Pallas kernels, body(): pl.pallas_call(kernel, out_shape=outs, in_specs=[pl.BlockSpec(memory_spac...  117 us

profile of v4, /device:TPU:6, one launch (start us, length us, event | category | flops | bytes accessed | tf_op | source)
XLA Modules:
  0.0 119.6 jit_solution(12136840030294828647)
XLA Ops:
  0.6 116.8 %shard_map.222 = (bf16[128,1024]{1,0:T(8,128)(2,1)}, bf16[128,1024]{1,0:T(8,128)(2,1)}, f32[16,128]{1,0:T(8,128)}, f32[16,128]{1,0:T(8,128)}, f32[8,128]{1,0:T(8...) custom-call(bf16[128,512]{1,0:T(8,128)(2,1)} %refs_0_.1, ...), custom_call_target="tpu_custom_call" | custom-call | tf_op jit(solution)/shard_map/pallas_call | solution.py:679
  117.4 2.1 %shard_map.223 = (bf16[128,1024]{1,0:T(8,128)(2,1)}, bf16[128,1024]{1,0:T(8,128)(2,1)}, f32[16,128]{1,0:T(8,128)}, f32[16,128]{1,0:T(8,128)}, f32[8,128]{1,0:T(8...) custom-call(bf16[128,1024]{1,0:T(8,128)(2,1)} %get-tuple-element.30., ...), custom_call_target="tpu_custom_call" | custom-call | tf_op jit(solution)/shard_map/pallas_call | solution.py:724

commit v5 on v4

--- a/solution.py
+++ b/solution.py
@@ -16,7 +16,8 @@
 OWN = TOK // SIDE
 CHUNKS = 4
 ROWS = NSTATE // CHUNKS
-EARLY = 80
+EARLY = 40
+LATE = 24
 MESH = pl.DeviceIdType.MESH
 F32 = jnp.float32
 BF16 = jnp.bfloat16
@@ -58,6 +59,9 @@
     return copy
 
 
+FARTHEST = (4, 3, 5, 2, 6, 1, 7)
+
+
 class Copies:
     def __init__(self, send_sem, recv_sem):
         self.send_sem, self.recv_sem, self.used, self.all = send_sem, recv_sem, 0, []
@@ -70,11 +74,11 @@
         return copy
 
     def exchange(self, kind, source, target):
-        started = []
-        for step in range(1, SIDE):
+        started = {}
+        for step in FARTHEST:
             device, place = along(kind, step)
-            started.append(self.start(device, source(place), target))
-        return started
+            started[step] = self.start(device, source(place), target)
+        return [started[step] for step in range(1, SIDE)]
 
     def left(self):
         for copy in self.all:
@@ -227,12 +231,14 @@
         self.copies, self.first, self.second = copies, first, second
         self.own, self.first_in, self.second_out, self.second_in, self.all = refs
         self.part, self.other = own_place(first), own_place(second)
-
-    def to_owner(self):
-        self.flight = self.copies.exchange(
-            self.first, lambda place: self.own.at[place], self.first_in.at[self.part]
-        )
-        self.first_in[self.part] = self.own[self.part]
+        self.flight = []
+
+    def to_owner(self, start, rows):
+        at = pl.ds(start, rows)
+        self.flight += self.copies.exchange(
+            self.first, lambda place: self.own.at[place, at], self.first_in.at[self.part, at]
+        )
+        self.first_in[self.part, at] = self.own[self.part, at]
 
     def to_line(self):
         arrived(self.flight)
@@ -270,7 +276,7 @@
     return total
 
 
-COPIES = 2 + 2 * 3 * CHUNKS * 7 + 5 * 7 + 5 * 3 * 7
+COPIES = 2 + 2 * 3 * CHUNKS * 7 + 5 * 7 + 2 * 7 * 7
 WIDE = 13
 INPUTS = 14
 FETCH_ORDER = (1, 5, 3, 6, 11, 12, 8, 0, 4, 2, 13, 10, 7, 9)
@@ -294,8 +300,7 @@
     (gconv_ref, ggate_ref, gb_ref, gc_ref, gl_ref, glayer_ref, ga_in_ref, gb_in_ref, ga_out_ref,
      gb_out_ref) = results
     fold_refs, back_refs = take(7), take(7)
-    early_refs = take(5)
-    conv_refs, low_refs = (take(5), take(5)), (take(5), take(5))
+    early_refs, late_refs = (take(5), take(5)), (take(5), take(5))
     (
         pre3, act3, slope3, y3, outer3, mix3, decay3, weighted3, gs3, dgs3, gssd3, ecum3, toend3,
     ) = take(WIDE)
@@ -334,8 +339,7 @@
             loads[next(i for i, place in enumerate(places) if place is ref)].wait()
 
     fetched(conv_ref)
-    pl.semaphore_wait(barrier, greeted)
-    tail = copies.start(along("seq", 1)[0], conv_ref.at[TOK - 16 : TOK], halo)
+    ext[0:8] = jnp.zeros((8, SIDE * HDIM), F32)
     ext[8 : TOK + 8] = conv_ref[...].astype(F32)
     rows_at = lax.broadcasted_iota(jnp.int32, (TOK, TOK), 0)
     cols_at = lax.broadcasted_iota(jnp.int32, (TOK, TOK), 1)
@@ -350,28 +354,33 @@
         fold_refs[0][h, 0:8] = total
         back_refs[0][h, 0:8] = total
     b_turned = b_ref[...].astype(F32).T.astype(BF16)
-    tail.wait_recv()
-    before = halo[...].astype(F32)[8:16]
-    ext[0:8] = jnp.where(seq > 0, before, 0.0)
     fold = Fold(copies, fold_refs, False)
 
-    def local_state(h):
+    def activate(h, rows):
         at = lanes(h)
         taps = tap_ref[:, at].astype(F32)
-        pre = ext[5 : 5 + TOK, at] * taps[0:1]
+        pre = ext[5 : 5 + rows, at] * taps[0:1]
         for k in range(1, KCONV):
-            pre = pre + ext[5 + k : 5 + k + TOK, at] * taps[k : k + 1]
+            pre = pre + ext[5 + k : 5 + k + rows, at] * taps[k : k + 1]
         sig = sigmoid(pre)
-        act = pre * sig
-        act3[h] = act
-        slope3[h] = sig * (1.0 + pre * (1.0 - sig))
-        fold.own[h, 8 : 8 + NSTATE] = left_exact(b_turned, act * toend3[h])
-
-    for step in range(1, SIDE + 1):
+        act3[h, 0:rows] = pre * sig
+        slope3[h, 0:rows] = sig * (1.0 + pre * (1.0 - sig))
+
+    each_head(lambda h: activate(h, TOK))
+    pl.semaphore_wait(barrier, greeted)
+    tail = copies.start(along("seq", 1)[0], conv_ref.at[TOK - 16 : TOK], halo)
+    tail.wait_recv()
+    ext[0:8] = jnp.where(seq > 0, halo[...].astype(F32)[8:16], 0.0)
+
+    def local_state(h):
+        activate(h, 8)
+        fold.own[h, 8 : 8 + NSTATE] = left_exact(b_turned, act3[h] * toend3[h])
+
+    for step in FARTHEST + (SIDE,):
         local_state(lax.rem(fold.col + step, SIDE))
         fold.to_owner(0, step)
     for chunk in range(1, CHUNKS):
-        for step in range(1, SIDE + 1):
+        for step in FARTHEST + (SIDE,):
             fold.to_owner(chunk, step)
 
     fetched(up_out_ref, og_ref, down_in_ref, x_ref)
@@ -473,23 +482,28 @@
         back.own[h, 8 : 8 + NSTATE] = left_exact(c_turned, gssd * ecum3[h])
 
     back = Fold(copies, back_refs, True)
-    for step in range(1, SIDE + 1):
+    for step in FARTHEST + (SIDE,):
         mixer_gradient(lax.rem(back.col + step, SIDE))
         back.to_owner(0, step)
     for chunk in range(1, CHUNKS):
-        for step in range(1, SIDE + 1):
+        for step in FARTHEST + (SIDE,):
             back.to_owner(chunk, step)
 
     scale = ADAPTER_SCALE / (SIDE * SIDE * TOK)
-    early = TokenSum(copies, early_refs, "z", "y")
+    axes = (("z", "y"), ("y", "z"))
+    early = [TokenSum(copies, refs, *axis) for refs, axis in zip(early_refs, axes)]
 
     def early_parts(h, low):
         at = lanes(h)
         ggate = pre3[h]
         ggate_ref[:, at] = ggate.astype(BF16)
-        early.own[h, 0:RANK] = scale * both(low_in_turned, ggate)
+        grad = scale * both(low_in_turned, ggate)
+        early[0].own[h, 0:16] = grad[0:16]
+        early[1].own[h, 0:16] = grad[16:32]
         normed = y3[h] * gs3[h] * gain_ref[:, at] * inv
-        early.own[h, RANK : 2 * RANK] = scale * both(back_out_turned, normed)
+        grad = scale * both(back_out_turned, normed)
+        early[0].own[h, 16:32] = grad[0:16]
+        early[1].own[h, 16:32] = grad[16:32]
         return low + left_exact(up_in_ref[1, :, at], ggate, nt)
 
     low_gate = lax.fori_loop(0, SIDE, early_parts, jnp.zeros((RANK, TOK), F32))
@@ -497,11 +511,12 @@
     low_out_turned = head_total(out_all) * inv_row
     grad_b_out = scale * right_exact(low_out_turned, og_ref[...])
     for part in range(SIDE):
-        early.own[part, 2 * RANK : 2 * RANK + 16] = grad_b_out[
-            16 * (part % 2) : 16 * (part % 2) + 16, HDIM * (part // 2) : HDIM * (part // 2 + 1)
-        ]
+        at = slice(HDIM * (part // 2), HDIM * (part // 2 + 1))
+        for sums, first_row in zip(early, (8 * (part % 2), 16 + 8 * (part % 2))):
+            sums.own[part, 32:40] = grad_b_out[first_row : first_row + 8, at]
     store(ggate_ref)
-    early.to_owner()
+    for sums in early:
+        sums.to_owner(0, EARLY)
 
     gc_acc[...] = jnp.zeros((TOK, NSTATE), F32)
     dg_acc[...] = jnp.zeros((TOK, TOK), F32)
@@ -527,7 +542,8 @@
     for chunk in range(CHUNKS - 1):
         back.to_all(chunk)
     back.to_all(CHUNKS - 1)
-    early.to_line()
+    for sums in early:
+        sums.to_line()
     state_grad = back.out
 
     for step in NEAREST:
@@ -550,12 +566,11 @@
         gext[0:TOK, lanes(h)] = (mix3[h] + into) * slope3[h]
 
     each_head(state_gradient)
-    early.to_all()
+    for sums in early:
+        sums.to_all()
     rim.wait_recv()
     gext[TOK : TOK + 8] = jnp.where(seq < SIDE * SIDE - 1, halo_g[...], 0.0)
-    axes = (("z", "y"), ("y", "z"))
-    conv_sums = [TokenSum(copies, refs, *axis) for refs, axis in zip(conv_refs, axes)]
-    low_sums = [TokenSum(copies, refs, *axis) for refs, axis in zip(low_refs, axes)]
+    late = [TokenSum(copies, refs, *axis) for refs, axis in zip(late_refs, axes)]
 
     def conv_gradient(h, low):
         at = lanes(h)
@@ -573,12 +588,12 @@
 
     def conv_parts(h):
         grad = scale * both(low_in_turned, y3[h])
-        conv_sums[0].own[h] = grad[0:16]
-        conv_sums[1].own[h] = grad[16:32]
+        late[0].own[h, 0:16] = grad[0:16]
+        late[1].own[h, 0:16] = grad[16:32]
 
     each_head(conv_parts)
-    for sums in conv_sums:
-        sums.to_owner()
+    for sums in late:
+        sums.to_owner(0, 16)
     store(gconv_ref)
     dcum = turned(
         jnp.concatenate(
@@ -594,10 +609,10 @@
     grad_a_in = scale * right_exact(back_in_turned, x_ref[...])
     for part in range(SIDE):
         at = slice(HDIM * (part // 2), HDIM * (part // 2 + 1))
-        for sums, first_row in zip(low_sums, (8 * (part % 2), 16 + 8 * (part % 2))):
-            sums.own[part] = grad_a_in[first_row : first_row + 8, at]
-    for sums in low_sums:
-        sums.to_owner()
+        for sums, first_row in zip(late, (8 * (part % 2), 16 + 8 * (part % 2))):
+            sums.own[part, 16:24] = grad_a_in[first_row : first_row + 8, at]
+    for sums in late:
+        sums.to_owner(16, 8)
     for part in range(SIDE):
         bc_own[part, 0:OWN] = gb_acc[OWN * part : OWN * (part + 1)]
         bc_own[part, OWN : 2 * OWN] = gc_acc[OWN * part : OWN * (part + 1)]
@@ -605,33 +620,37 @@
     bc_all[head] = bc_own[head]
     back_in = turned(jnp.concatenate([back_in_turned, pad], axis=0))[:, 0:RANK]
     glayer_ref[...] = (ADAPTER_SCALE * right_exact(back_in, down_in_ref[...])).astype(BF16)
-    for sums in conv_sums + low_sums:
+    for sums in late:
         sums.to_line()
-    early.end()
+    for sums in early:
+        sums.end()
     for part in range(SIDE):
         at = slice(HDIM * part, HDIM * (part + 1))
-        gb_in_ref[1, :, at] = early.all[part, 0:RANK]
-        ga_out_ref[:, at] = early.all[part, RANK : 2 * RANK]
-        gb_out_ref[
-            16 * (part % 2) : 16 * (part % 2) + 16, HDIM * (part // 2) : HDIM * (part // 2 + 1)
-        ] = early.all[part, 2 * RANK : 2 * RANK + 16]
+        for half, sums in enumerate(early):
+            rows = slice(16 * half, 16 * half + 16)
+            gb_in_ref[1, rows, at] = sums.all[part, 0:16]
+            ga_out_ref[rows, at] = sums.all[part, 16:32]
+            first_row = 16 * half + 8 * (part % 2)
+            gb_out_ref[
+                first_row : first_row + 8, HDIM * (part // 2) : HDIM * (part // 2 + 1)
+            ] = sums.all[part, 32:40]
     store(ga_out_ref, gb_out_ref)
     arrived(rows_out)
     sums = head_total(bc_all)
     gb_ref[...] = sums[0:OWN]
     gc_ref[...] = sums[OWN : 2 * OWN]
     store(glayer_ref, gb_ref, gc_ref)
-    for sums in conv_sums + low_sums:
+    for sums in late:
         sums.to_all()
-    for sums in conv_sums + low_sums:
+    for sums in late:
         sums.end()
     for part in range(SIDE):
         at = slice(HDIM * part, HDIM * (part + 1))
-        gb_in_ref[0, 0:16, at] = conv_sums[0].all[part]
-        gb_in_ref[0, 16:32, at] = conv_sums[1].all[part]
+        gb_in_ref[0, 0:16, at] = late[0].all[part, 0:16]
+        gb_in_ref[0, 16:32, at] = late[1].all[part, 0:16]
         at = slice(HDIM * (part // 2), HDIM * (part // 2 + 1))
-        for sums, first_row in zip(low_sums, (8 * (part % 2), 16 + 8 * (part % 2))):
-            ga_in_ref[first_row : first_row + 8, at] = sums.all[part]
+        for sums, first_row in zip(late, (8 * (part % 2), 16 + 8 * (part % 2))):
+            ga_in_ref[first_row : first_row + 8, at] = sums.all[part, 16:24]
     store(gb_in_ref, ga_in_ref)
     copies.left()
     for copy in stores:
@@ -687,10 +706,9 @@
         + fold_scratch()
         + fold_scratch()
         + token_sum_scratch(EARLY)
-        + token_sum_scratch(16)
-        + token_sum_scratch(16)
-        + token_sum_scratch(8)
-        + token_sum_scratch(8)
+        + token_sum_scratch(EARLY)
+        + token_sum_scratch(LATE)
+        + token_sum_scratch(LATE)
         + [pltpu.VMEM((SIDE, TOK, HDIM), F32) for _ in range(WIDE)]
         + [
             pltpu.VMEM((TOK + 8, wide), F32),

time: 120 us -> 115 us (0.958)
  Pallas kernels: 119 us -> 114 us
    pallas_call x1, Pallas kernels: 117 us -> 112 us  [body(): pl.pallas_call(kernel, out_shape=outs, in_specs=[pl.BlockSpec(memory_spac...]
where the time goes in v5:
time: 115 us
  Pallas kernels  114 us (99%)
    pallas_call x1, Pallas kernels, body(): pl.pallas_call(kernel, out_shape=outs, in_specs=[pl.BlockSpec(memory_spac...  112 us

profile of v5, /device:TPU:6, one launch (start us, length us, event | category | flops | bytes accessed | tf_op | source)
XLA Modules:
  0.0 114.8 jit_solution(13938717202500738895)
XLA Ops:
  0.6 112.0 %shard_map.222 = (bf16[128,1024]{1,0:T(8,128)(2,1)}, bf16[128,1024]{1,0:T(8,128)(2,1)}, f32[16,128]{1,0:T(8,128)}, f32[16,128]{1,0:T(8,128)}, f32[8,128]{1,0:T(8...) custom-call(bf16[128,512]{1,0:T(8,128)(2,1)} %refs_0_.1, ...), custom_call_target="tpu_custom_call" | custom-call | tf_op jit(solution)/shard_map/pallas_call | solution.py:698
  112.6 2.1 %shard_map.223 = (bf16[128,1024]{1,0:T(8,128)(2,1)}, bf16[128,1024]{1,0:T(8,128)(2,1)}, f32[16,128]{1,0:T(8,128)}, f32[16,128]{1,0:T(8,128)}, f32[8,128]{1,0:T(8...) custom-call(bf16[128,1024]{1,0:T(8,128)(2,1)} %get-tuple-element.30., ...), custom_call_target="tpu_custom_call" | custom-call | tf_op jit(solution)/shard_map/pallas_call | solution.py:742

commit v6 on v5

--- a/solution.py
+++ b/solution.py
@@ -566,8 +566,6 @@
         gext[0:TOK, lanes(h)] = (mix3[h] + into) * slope3[h]
 
     each_head(state_gradient)
-    for sums in early:
-        sums.to_all()
     rim.wait_recv()
     gext[TOK : TOK + 8] = jnp.where(seq < SIDE * SIDE - 1, halo_g[...], 0.0)
     late = [TokenSum(copies, refs, *axis) for refs, axis in zip(late_refs, axes)]
@@ -594,6 +592,8 @@
     each_head(conv_parts)
     for sums in late:
         sums.to_owner(0, 16)
+    for sums in early:
+        sums.to_all()
     store(gconv_ref)
     dcum = turned(
         jnp.concatenate(

time: 115 us -> 114 us (level)
    pallas_call x1, Pallas kernels: 112 us -> 111 us  [body(): pl.pallas_call(kernel, out_shape=outs, in_specs=[pl.BlockSpec(memory_spac...]
where the time goes in v6:
time: 114 us
  Pallas kernels  113 us (99%)
    pallas_call x1, Pallas kernels, body(): pl.pallas_call(kernel, out_shape=outs, in_specs=[pl.BlockSpec(memory_spac...  111 us

profile of v6, /device:TPU:6, one launch (start us, length us, event | category | flops | bytes accessed | tf_op | source)
XLA Modules:
  0.0 113.6 jit_solution(8301139391285209215)
XLA Ops:
  0.6 110.8 %shard_map.222 = (bf16[128,1024]{1,0:T(8,128)(2,1)}, bf16[128,1024]{1,0:T(8,128)(2,1)}, f32[16,128]{1,0:T(8,128)}, f32[16,128]{1,0:T(8,128)}, f32[8,128]{1,0:T(8...) custom-call(bf16[128,512]{1,0:T(8,128)(2,1)} %refs_0_.1, ...), custom_call_target="tpu_custom_call" | custom-call | tf_op jit(solution)/shard_map/pallas_call | solution.py:698
  111.5 2.1 %shard_map.223 = (bf16[128,1024]{1,0:T(8,128)(2,1)}, bf16[128,1024]{1,0:T(8,128)(2,1)}, f32[16,128]{1,0:T(8,128)}, f32[16,128]{1,0:T(8,128)}, f32[8,128]{1,0:T(8...) custom-call(bf16[128,1024]{1,0:T(8,128)(2,1)} %get-tuple-element.30., ...), custom_call_target="tpu_custom_call" | custom-call | tf_op jit(solution)/shard_map/pallas_call | solution.py:742
